TPU v7x, 32 devices: a whole 2x2x4 slice. The times are simulated.
32 devices in a mesh: lat: 4 (over z), lon: 8 (over y, x, core).
Axes of the slice: x: 2, y: 2, z: 4, core: 2. Of those that a mesh axis runs over, the one named last changes fastest.
Arguments:
- state_grid: bfloat16 [24, 672, 192], P('lat', 'lon'), may hold values from -6 to 6
- norm_gain: float32 [192], replicated, may hold values from 0.1 to 1.9
- w_qkv: bfloat16 [192, 576], replicated, may hold values from -0.4375 to 0.4375
- w_proj: bfloat16 [192, 192], replicated, may hold values from -1.25 to 1.25
- bias_table: float32 [8, 6, 253], replicated, may hold values from -6 to 300
- window_kind: int32 [4, 56], replicated, may hold values from 0 to 7
- cotangent: bfloat16 [24, 672, 192], P('lat', 'lon'), may hold values from -6 to 6
Outputs:
- out_field: bfloat16 [24, 672, 192], P('lat', 'lon')
- d_field: bfloat16 [24, 672, 192], P('lat', 'lon')
- qkv_grad: float32 [192, 576], replicated
- proj_grad: float32 [192, 192], replicated
- table_grad: float32 [8, 6, 253], replicated
- gain_grad: float32 [192], replicated
All inputs are finite; a program needn't handle non-finite values.
Results may differ from a plain program's by a relative error of at most 0.009.
Values may be sent and summed in bfloat16 or wider, within the bound.
A program may use at most 64 MiB of HBM per device.

v0:
```python
import jax
import jax.numpy as jnp
from jax import lax
from jax.sharding import PartitionSpec as P

HEADS = 6
WIN_LAT = 6
WIN_LON = 12


norm_eps = 1e-05
clip_eps = 1e-06
clip_level = 1.0
masked_score = -1e30
highest = lax.Precision.HIGHEST


def shifted(value, axis, steps):
    count = lax.axis_size(axis)
    pairs = [(source, (source + steps) % count) for source in range(count)]
    return lax.ppermute(value, axis, pairs)


def relation_onehot(win_lat, win_lon):
    position = jnp.arange(win_lat * win_lon, dtype=jnp.int32)
    row_of = position // win_lon
    column = position % win_lon
    offset = (row_of[:, None] - row_of[None, :] + win_lat - 1) * (2 * win_lon - 1) + (
        column[:, None] - column[None, :] + win_lon - 1
    )
    extent = (2 * win_lat - 1) * (2 * win_lon - 1)
    return (offset.reshape(-1)[:, None] == jnp.arange(extent, dtype=jnp.int32)[None, :]).astype(
        jnp.float32
    )


def to_windows(source, win_lat, win_lon):
    rows_all, cols_all, channels = source.shape
    source = source.reshape(rows_all // win_lat, win_lat, cols_all // win_lon, win_lon, channels)
    return source.transpose(0, 2, 1, 3, 4).reshape(-1, win_lat * win_lon, channels)


def from_windows(windows, rows_all, cols_all, win_lat, win_lon):
    channels = windows.shape[-1]
    source = windows.reshape(rows_all // win_lat, cols_all // win_lon, win_lat, win_lon, channels)
    return source.transpose(0, 2, 1, 3, 4).reshape(rows_all, cols_all, channels)


def window_bias(bias_table, kinds_flat, onehot_rel, positions):
    kind_count, heads_n, extent = bias_table.shape
    spread = jnp.einsum(
        "ke,pe->kp",
        bias_table.reshape(kind_count * heads_n, extent),
        onehot_rel,
        precision=highest,
        preferred_element_type=jnp.float32,
    )
    kind_onehot = (kinds_flat[:, None] == jnp.arange(kind_count, dtype=jnp.int32)[None, :]).astype(
        jnp.float32
    )
    per_window = jnp.dot(
        kind_onehot,
        spread.reshape(kind_count, heads_n * positions * positions),
        precision=highest,
        preferred_element_type=jnp.float32,
    )
    return (per_window.reshape(-1, heads_n, positions, positions), kind_onehot)


def attend_forward(x_windows, norm_gain, w_qkv, w_proj, bias_win, allowed):
    count, positions, channels = x_windows.shape
    head_size = channels // HEADS
    inv_sqrt = head_size ** (-0.5)
    flat_rows = x_windows.reshape(-1, channels).astype(jnp.float32)
    centre = flat_rows - jnp.mean(flat_rows, axis=-1, keepdims=True)
    inverse = lax.rsqrt(jnp.mean(centre * centre, axis=-1, keepdims=True) + norm_eps)
    unit_rows = centre * inverse
    normed = (unit_rows * norm_gain).astype(jnp.bfloat16)
    qkv_rows = jnp.dot(normed, w_qkv, preferred_element_type=jnp.float32).astype(jnp.bfloat16)
    parts_qkv = qkv_rows.reshape(count, positions, 3, HEADS, head_size)
    queries = parts_qkv[:, :, 0]
    keys_in = parts_qkv[:, :, 1]
    values_in = parts_qkv[:, :, 2]
    scores = (
        jnp.einsum("wihd,wjhd->whij", queries, keys_in, preferred_element_type=jnp.float32)
        * inv_sqrt
        + bias_win
    )
    scores = jnp.where(allowed, scores, masked_score)
    soft_probs = jax.nn.softmax(scores, axis=-1)
    probs_low = soft_probs.astype(jnp.bfloat16)
    mixed_rows = jnp.einsum(
        "whij,wjhd->wihd", probs_low, values_in, preferred_element_type=jnp.float32
    )
    mixed_rows = mixed_rows.astype(jnp.bfloat16).reshape(-1, channels)
    branch = jnp.dot(mixed_rows, w_proj, preferred_element_type=jnp.float32).astype(jnp.bfloat16)
    saved = (
        normed,
        unit_rows,
        inverse,
        queries,
        keys_in,
        values_in,
        soft_probs,
        probs_low,
        mixed_rows,
    )
    return (saved, branch)


def attend_backward(
    saved, g_windows, keep_win, w_qkv, w_proj, norm_gain, kind_onehot, onehot_rel, table_dims
):
    normed, unit_rows, inverse, queries, keys_in, values_in, soft_probs, probs_low, mixed_rows = (
        saved
    )
    count, heads_n, positions = (soft_probs.shape[0], soft_probs.shape[1], soft_probs.shape[2])
    channels = normed.shape[1]
    head_size = channels // heads_n
    inv_sqrt = head_size ** (-0.5)
    flat_g = g_windows.reshape(-1, channels)
    keep_rows = keep_win.reshape(-1, 1)
    keep_low = keep_rows.astype(jnp.bfloat16)
    grad_proj = jnp.einsum(
        "nc,nd->cd", mixed_rows * keep_low, flat_g, preferred_element_type=jnp.float32
    )
    d_mixed = jnp.einsum("nd,cd->nc", flat_g, w_proj, preferred_element_type=jnp.float32).astype(
        jnp.bfloat16
    )
    d_mixed = d_mixed.reshape(count, positions, heads_n, head_size)
    d_probs = jnp.einsum("wihd,wjhd->whij", d_mixed, values_in, preferred_element_type=jnp.float32)
    d_values = jnp.einsum(
        "whij,wihd->wjhd", probs_low, d_mixed, preferred_element_type=jnp.float32
    ).astype(jnp.bfloat16)
    d_scores = soft_probs * (d_probs - jnp.sum(soft_probs * d_probs, axis=-1, keepdims=True))
    d_scores_low = d_scores.astype(jnp.bfloat16)
    d_queries = (
        jnp.einsum("whij,wjhd->wihd", d_scores_low, keys_in, preferred_element_type=jnp.float32)
        * inv_sqrt
    ).astype(jnp.bfloat16)
    d_keys = (
        jnp.einsum("whij,wihd->wjhd", d_scores_low, queries, preferred_element_type=jnp.float32)
        * inv_sqrt
    ).astype(jnp.bfloat16)
    d_qkv = jnp.stack([d_queries, d_keys, d_values], axis=2).reshape(-1, 3 * channels)
    grad_qkv = jnp.einsum("nc,nd->cd", normed * keep_low, d_qkv, preferred_element_type=jnp.float32)
    d_normed = jnp.einsum("nd,cd->nc", d_qkv, w_qkv, preferred_element_type=jnp.float32)
    grad_gain = jnp.sum(d_normed * unit_rows * keep_rows, axis=0)
    d_unit = d_normed * norm_gain
    d_path = inverse * (
        d_unit
        - jnp.mean(d_unit, axis=-1, keepdims=True)
        - unit_rows * jnp.mean(d_unit * unit_rows, axis=-1, keepdims=True)
    )
    d_path = d_path.astype(jnp.bfloat16)
    query_keep = keep_win.reshape(count, 1, positions, 1)
    by_kind = jnp.einsum(
        "wk,wx->kx",
        kind_onehot,
        (d_scores * query_keep).reshape(count, -1),
        precision=highest,
        preferred_element_type=jnp.float32,
    )
    grad_table = jnp.dot(
        by_kind.reshape(-1, positions * positions),
        onehot_rel,
        precision=highest,
        preferred_element_type=jnp.float32,
    )
    return (d_path, (grad_qkv, grad_proj, grad_table.reshape(table_dims), grad_gain))


def shifted_pair(source, half_lat, half_lon):
    upper = shifted(source[:half_lat], "lat", -1)
    stacked = jnp.concatenate([source[half_lat:], upper], axis=0)
    right_side = shifted(stacked[:, :half_lon], "lon", -1)
    return jnp.concatenate([stacked[:, half_lon:], right_side], axis=1)


def unshift_pair(block, half_lat, half_lon):
    trailing = shifted(block[:, -half_lon:], "lon", 1)
    placed = jnp.concatenate([trailing, block[:, :-half_lon]], axis=1)
    lower = shifted(placed[-half_lat:], "lat", 1)
    return jnp.concatenate([lower, placed[:-half_lat]], axis=0)


def clip_rms(gradient):
    return gradient * jnp.minimum(
        1.0, clip_level * lax.rsqrt(jnp.mean(gradient * gradient) + clip_eps)
    )


def on_device(state_grid, norm_gain, w_qkv, w_proj, bias_table, window_kind, cotangent):
    rows_dev, cols_dev, channels = state_grid.shape
    half_lat = WIN_LAT // 2
    half_lon = WIN_LON // 2
    positions = WIN_LAT * WIN_LON
    lat_index = lax.axis_index("lat")
    lon_index = lax.axis_index("lon")
    rows_all = rows_dev * lax.axis_size("lat")
    onehot_rel = relation_onehot(WIN_LAT, WIN_LON)
    band_start = lat_index * (rows_dev // WIN_LAT)
    sector_start = lon_index * (cols_dev // WIN_LON)
    first_row = lat_index * rows_dev + half_lat
    types_block = lax.dynamic_slice(
        window_kind, (band_start, sector_start), (rows_dev // WIN_LAT, cols_dev // WIN_LON)
    )
    keep_grid = jnp.ones((rows_dev, cols_dev), jnp.float32)
    joint = jnp.concatenate([state_grid, cotangent], axis=2)
    block_joint = shifted_pair(joint, half_lat, half_lon)
    block_x = block_joint[:, :, :channels]
    block_g = block_joint[:, :, channels:]
    block_rows, block_cols = (block_x.shape[0], block_x.shape[1])
    row_ids = (first_row + jnp.arange(block_rows, dtype=jnp.int32)) % rows_all
    labels = (row_ids + half_lat) // WIN_LAT
    label_grid = jnp.broadcast_to(labels[:, None, None], (block_rows, block_cols, 1))
    label_win = to_windows(label_grid, WIN_LAT, WIN_LON)[:, :, 0]
    allowed = (label_win[:, :, None] == label_win[:, None, :])[:, None]
    keep_win = to_windows(keep_grid[:, :, None], WIN_LAT, WIN_LON)[:, :, 0]
    bias_win, kind_onehot = window_bias(bias_table, types_block.reshape(-1), onehot_rel, positions)
    saved, branch = attend_forward(
        to_windows(block_x, WIN_LAT, WIN_LON), norm_gain, w_qkv, w_proj, bias_win, allowed
    )
    branch_grid = from_windows(
        branch.reshape(-1, positions, channels), block_rows, block_cols, WIN_LAT, WIN_LON
    )
    g_windows = to_windows(block_g, WIN_LAT, WIN_LON)
    d_path, grads = attend_backward(
        saved,
        g_windows,
        keep_win,
        w_qkv,
        w_proj,
        norm_gain,
        kind_onehot,
        onehot_rel,
        bias_table.shape,
    )
    path_grid = from_windows(
        d_path.reshape(-1, positions, channels), block_rows, block_cols, WIN_LAT, WIN_LON
    )
    both_own = unshift_pair(jnp.concatenate([branch_grid, path_grid], axis=2), half_lat, half_lon)
    branch_own = both_own[:, :, :channels]
    path_own = both_own[:, :, channels:]
    out_field = (state_grid.astype(jnp.float32) + branch_own.astype(jnp.float32)).astype(
        jnp.bfloat16
    )
    d_field = (cotangent.astype(jnp.float32) + path_own.astype(jnp.float32)).astype(jnp.bfloat16)
    grad_qkv, grad_proj, grad_table, grad_gain = grads
    summed = lax.psum((grad_qkv, grad_proj, grad_table, grad_gain), ("lat", "lon"))
    qkv_grad = clip_rms(summed[0])
    proj_grad = clip_rms(summed[1])
    table_grad = clip_rms(summed[2])
    gain_grad = clip_rms(summed[3])
    return (out_field, d_field, qkv_grad, proj_grad, table_grad, gain_grad)


def solution(mesh):
    in_specs = (P("lat", "lon", None), P(), P(), P(), P(), P(), P("lat", "lon", None))
    out_specs = (P("lat", "lon", None), P("lat", "lon", None), P(), P(), P(), P())
    return jax.shard_map(
        on_device, mesh=mesh, in_specs=in_specs, out_specs=out_specs, check_vma=False
    )
```

profile of v0, /device:TPU:0, one launch (start us, length us, event | category | flops | bytes accessed | tf_op | source)
XLA Modules:
  0.0 259.0 jit_solution(4553154303973583669)
XLA Ops:
  7.2 2.0 fusion.30
  9.2 5.1 %collective-permute-start = (bf16[3,84,384]{2,1,0:T(8,128)(2,1)}, bf16[3,84,384]{2,1,0:T(8,128)(2,1)S(1)}, u32[]{:S(2)}, u32[]{:S(2)}) collective-permute-start(bf16[3,84,384]{2,1,0:T(8,128)(2,1)} %get-tuple-element.17), channel_id=1, source_target_pairs={{0,24},{8,0},{16,8},{24,16},{1,25},{9,1},{17,9},{25,17},{2,26},{10... | collective-permute-start | bytes 580616 | tf_op jit(solution)/shard_map/ppermute | solution.py:21
  15.5 2.6 %convolution_bitcast_fusion = f32[48,5184]{1,0:T(8,128)S(1)} fusion(f32[48,253]{1,0:T(8,128)S(1)} %reshape.225, s32[5184]{0:T(1024)S(1)} %add.155), kind=kOutput, calls=%fused_computation.1 | convolution fusion | flops 756765504 | bytes 1064640 | tf_op jit(solution)/shard_map/ke,pe->kp/dot_general | solution.py:51
  18.9 2.7 %dot_general.63 = f32[6,72,72,8]{2,1,0,3:T(8,128)} reshape(f32[31104,8]{0,1:T(8,128)S(1)} %bitcast.82) | data formatting | bytes 1990656 | tf_op jit(solution)/shard_map/dot_general | solution.py:61
  22.3 2.8 %fusion.6 = f32[7,6,72,72]{3,0,2,1:T(8,128)S(1)} fusion(f32[6,72,72,8]{2,1,0,3:T(8,128)} %dot_general.63, s32[7]{0:T(128)S(1)} %dynamic-slice_bitcast_fusion), kind=kOutput, calls=%fused_computation.7 | convolution fusion | flops 20901944 | bytes 1866268 | tf_op jit(solution)/shard_map/dot_general | solution.py:61
  26.9 1.7 collective-permute-start.1
  37.8 2.3 fusion.43
  40.2 2.3 fusion.12
  42.5 1.9 copy.63
  45.7 2.0 convolution_convert_fusion.3
  47.7 1.9 fusion.45
  49.5 1.8 convolution_convert_fusion.4
  51.4 2.0 reshape.230
  53.4 2.3 fusion.13
  55.7 1.8 multiply_reduce_fusion
  64.2 2.2 reshape.233
  69.3 1.9 fusion.2
  72.9 37.5 %all-reduce = (f32[8,6,253]{2,0,1:T(8,128)S(1)}, f32[192]{0:T(256)S(1)}) all-reduce(f32[8,6,253]{2,0,1:T(8,128)S(1)} %fusion.2, f32[192]{0:T(256)S(1)} %get-tuple-element.6), channel_id=1, replica_groups=mesh['lat'=4,'lon'=8] {'lat','lon'}, use_global_device_ids=true, to_apply=%region_11.12 | all-reduce | flops 12336 | bytes 98688 | tf_op jit(solution)/shard_map/psum | solution.py:250
  114.7 3.0 %collective-permute-done.2 = bf16[6,6,384]{2,1,0:T(8,128)(2,1)S(1)} collective-permute-done((bf16[6,6,384]{2,1,0:T(8,128)(2,1)S(1)}, bf16[6,6,384]{2,1,0:T(8,128)(2,1)S(1)}, u32[]{:S(2)}, u32[]{:S(2)}) %collective-permute-start.2) | collective-permute-done | bytes 27680 | tf_op jit(solution)/shard_map/ppermute | solution.py:21
  117.9 2.8 %collective-permute-start.3 = (bf16[3,84,384]{2,1,0:T(8,128)(2,1)S(1)}, bf16[3,84,384]{2,1,0:T(8,128)(2,1)S(1)}, u32[]{:S(2)}, u32[]{:S(2)}) collective-permute-start(bf16[3,84,384]{2,1,0:T(8,128)(2,1)S(1)} %get-tuple-element.21), channel_id=1, source_target_pairs={{0,8},{8,16},{16,24},{24,0},{1,9},{9,17},{17,25},{25,1},{2,10},{10... | collective-permute-start | bytes 580616 | tf_op jit(solution)/shard_map/ppermute | solution.py:21
  121.3 5.2 %collective-permute-done.3 = bf16[3,84,384]{2,1,0:T(8,128)(2,1)S(1)} collective-permute-done((bf16[3,84,384]{2,1,0:T(8,128)(2,1)S(1)}, bf16[3,84,384]{2,1,0:T(8,128)(2,1)S(1)}, u32[]{:S(2)}, u32[]{:S(2)}) %collective-permute-start.3) | collective-permute-done | bytes 193568 | tf_op jit(solution)/shard_map/ppermute | solution.py:21
  127.5 117.3 %all-reduce.4.cloned.1.call-done = (f32[192,576]{1,0:T(8,128)}, f32[192,192]{1,0:T(8,128)}) async-done(((f32[192,576]{1,0:T(8,128)}, f32[192,192]{1,0:T(8,128)}), (f32[192,576]{1,0:T(8,128)}, f32[192,192]{1,0:T(8,128)})) %all-reduce.4.cloned.1.call-update) | async-done | bytes 589840 | tf_op jit(solution)/shard_map/psum | solution.py:250
  247.2 1.8 multiply_reduce_fusion.2
  249.6 1.8 broadcast_multiply_fusion
  (121 shorter events, 33.2 us)
Async XLA Ops:
  7.2 27.0 %copy-start = (bf16[192,576]{1,0:T(8,128)(2,1)S(1)}, bf16[192,576]{1,0:T(8,128)(2,1)}, u32[]{:S(2)}) copy-start(bf16[192,576]{1,0:T(8,128)(2,1)} %param.9) | copy-start | bytes 663556
  7.2 237.6 %all-reduce.4.cloned.1.call-start = ((), (), s32[]{:S(2)}) async-start(), calls=%async_computation | async-start | bytes 1376256 | tf_op jit(solution)/shard_map/psum | solution.py:250
  9.2 17.6 %collective-permute-start = (bf16[3,84,384]{2,1,0:T(8,128)(2,1)}, bf16[3,84,384]{2,1,0:T(8,128)(2,1)S(1)}, u32[]{:S(2)}, u32[]{:S(2)}) collective-permute-start(bf16[3,84,384]{2,1,0:T(8,128)(2,1)} %get-tuple-element.17), channel_id=1, source_target_pairs={{0,24},{8,0},{16,8},{24,16},{1,25},{9,1},{17,9},{25,17},{2,26},{10... | collective-permute-start | bytes 580616 | tf_op jit(solution)/shard_map/ppermute | solution.py:21
  14.7 0.9 copy-start.20
  26.9 3.3 %collective-permute-start.1 = (bf16[6,6,384]{2,1,0:T(8,128)(2,1)S(1)}, bf16[6,6,384]{2,1,0:T(8,128)(2,1)S(1)}, u32[]{:S(2)}, u32[]{:S(2)}) collective-permute-start(bf16[6,6,384]{2,1,0:T(8,128)(2,1)S(1)} %pad_maximum_fusion.6), channel_id=1, source_target_pairs={{0,7},{1,0},{2,1},{3,2},{4,3},{5,4},{6,5},{7,6},{8,15},{9,8},{10,9... | collective-permute-start | bytes 82952 | tf_op jit(solution)/shard_map/ppermute | solution.py:21
  35.6 1.6 copy-start.1
  36.5 1.4 copy-start.7
  40.2 2.3 copy-start.18
  53.4 2.3 copy-start.19
  57.4 1.0 copy-start.8
  58.4 1.3 copy-start.6
  60.8 2.3 copy-start.16
  63.3 3.0 %copy-start.10 = (bf16[7,72,1,6,32]{1,4,3,0,2:T(8,128)(2,1)S(1)}, bf16[7,72,1,6,32]{1,4,3,0,2:T(8,128)(2,1)}, u32[]{:S(2)}) copy-start(bf16[7,72,1,6,32]{1,4,3,0,2:T(8,128)(2,1)} %fusion.14) | copy-start | bytes 580612
  63.3 3.0 %copy-start.11 = (bf16[7,72,1,6,32]{1,4,3,0,2:T(8,128)(2,1)S(1)}, bf16[7,72,1,6,32]{1,4,3,0,2:T(8,128)(2,1)}, u32[]{:S(2)}) copy-start(bf16[7,72,1,6,32]{1,4,3,0,2:T(8,128)(2,1)} %fusion.15) | copy-start | bytes 580612
  63.3 3.0 %copy-start.17 = (bf16[7,72,1,6,32]{1,4,3,0,2:T(8,128)(2,1)S(1)}, bf16[7,72,1,6,32]{1,4,3,0,2:T(8,128)(2,1)}, u32[]{:S(2)}) copy-start(bf16[7,72,1,6,32]{1,4,3,0,2:T(8,128)(2,1)} %fusion.13) | copy-start | bytes 580612
  66.6 1.5 copy-start.2
  68.6 2.6 %copy-start.4 = (f32[504,192]{0,1:T(8,128)S(1)}, f32[504,192]{0,1:T(8,128)}, u32[]{:S(2)}) copy-start(f32[504,192]{0,1:T(8,128)} %copy-done.3) | copy-start | bytes 1161220
  69.3 2.4 copy-start.14
  112.3 1.0 copy-start.9
  113.2 13.3 %copy-start.12 = (bf16[6,84,192]{2,1,0:T(8,128)(2,1)S(1)}, bf16[6,84,192]{2,1,0:T(8,128)(2,1)}, u32[]{:S(2)}) copy-start(bf16[6,84,192]{2,1,0:T(8,128)(2,1)} %param.13) | copy-start | bytes 580612
  113.2 13.3 %copy-start.13 = (bf16[6,84,192]{2,1,0:T(8,128)(2,1)S(1)}, bf16[6,84,192]{2,1,0:T(8,128)(2,1)}, u32[]{:S(2)}) copy-start(bf16[6,84,192]{2,1,0:T(8,128)(2,1)} %param.7) | copy-start | bytes 580612
  113.3 4.3 %collective-permute-start.2 = (bf16[6,6,384]{2,1,0:T(8,128)(2,1)S(1)}, bf16[6,6,384]{2,1,0:T(8,128)(2,1)S(1)}, u32[]{:S(2)}, u32[]{:S(2)}) collective-permute-start(bf16[6,6,384]{2,1,0:T(8,128)(2,1)S(1)} %pad_maximum_fusion.5), channel_id=1, source_target_pairs={{0,1},{1,2},{2,3},{3,4},{4,5},{5,6},{6,7},{7,0},{8,9},{9,10},{10,1... | collective-permute-start | bytes 82952 | tf_op jit(solution)/shard_map/ppermute | solution.py:21
  117.9 8.6 %collective-permute-start.3 = (bf16[3,84,384]{2,1,0:T(8,128)(2,1)S(1)}, bf16[3,84,384]{2,1,0:T(8,128)(2,1)S(1)}, u32[]{:S(2)}, u32[]{:S(2)}) collective-permute-start(bf16[3,84,384]{2,1,0:T(8,128)(2,1)S(1)} %get-tuple-element.21), channel_id=1, source_target_pairs={{0,8},{8,16},{16,24},{24,0},{1,9},{9,17},{17,25},{25,1},{2,10},{10... | collective-permute-start | bytes 580616 | tf_op jit(solution)/shard_map/ppermute | solution.py:21
  244.8 6.6 %copy-start.15 = (f32[192,192]{1,0:T(8,128)S(1)}, f32[192,192]{1,0:T(8,128)}, u32[]{:S(2)}) copy-start(f32[192,192]{1,0:T(8,128)} %get-tuple-element.12) | copy-start | bytes 442372
  (4 other events, 3.1 us)
Sparse Core Ops, SparseCore 0:
  114.8 129.9 all-reduce.3
where the time goes:
time: 260 us; the launch traced here: 259 us
  waiting for transfers between devices  127 us (49%)
  blocking collectives  37.5 us (14%)
  local copies, waits for them, and re-layouts  26 us (10%)
  matrix products  25 us (10%)
  between operations  17.3 us (7%)
  other arithmetic  16.6 us (6%)
  starting transfers between devices  9.66 us (4%)
    psum x1, waiting for transfers between devices, on_device(): lax.psum((grad_qkv, grad_proj, grad_table, grad_gain), ('lat', 'lon'))  117 us
    psum x1, blocking collectives, on_device(): lax.psum((grad_qkv, grad_proj, grad_table, grad_gain), ('lat', 'lon'))  37.5 us
    ppermute x4, waiting for transfers between devices, shifted(): return lax.ppermute(value, axis, pairs)  9.65 us
    ppermute x4, starting transfers between devices, shifted(): return lax.ppermute(value, axis, pairs)  9.62 us
  transfers between devices with their start and end apart: 5, of which 4 were waited for; matrix products, arithmetic and copies ran while one was open for 6% of the time, Pallas kernels for 0%

commit v1 on v0

v1 whole, which is shorter than its diff:
```python
import functools

import jax
import jax.numpy as jnp
from jax import lax
from jax.experimental import pallas as pl
from jax.experimental.pallas import tpu as pltpu
from jax.sharding import PartitionSpec as P

HEADS = 6
WIN_LAT = 6
WIN_LON = 12
HALF_LAT = 3
HALF_LON = 6
PAD = 8
SPAN = 2 * WIN_LON - 1
TOP = (WIN_LAT - 1) * SPAN + WIN_LON - 1

norm_eps = 1e-05
clip_eps = 1e-06
masked_score = -1e30
f32 = jnp.float32
bf16 = jnp.bfloat16
MESH = pl.DeviceIdType.MESH
VM = pl.BlockSpec(memory_space=pltpu.VMEM)


def nt(a, b):
    return lax.dot_general(a, b, (((1,), (1,)), ((), ())), preferred_element_type=f32)


def tn(a, b):
    return lax.dot_general(a, b, (((0,), (0,)), ((), ())), preferred_element_type=f32)


def nn(a, b):
    return jnp.dot(a, b, preferred_element_type=f32)


def halo_kernel(nlat, nlon, own_ref, out_ref, sends, recvs, local):
    lat = lax.axis_index("lat")
    lon = lax.axis_index("lon")
    last = own_ref.shape[1] - 1
    up, down = lax.rem(lat + nlat - 1, nlat), lax.rem(lat + 1, nlat)
    left, right = lax.rem(lon + nlon - 1, nlon), lax.rem(lon + 1, nlon)
    barrier = pltpu.get_barrier_semaphore()
    for who in ((down, lon), (lat, right), (down, right)):
        pl.semaphore_signal(barrier, inc=1, device_id=who, device_id_type=MESH)
    pl.semaphore_wait(barrier, 3)
    top = pl.ds(0, HALF_LAT)
    bottom = pl.ds(HALF_LAT, HALF_LAT)
    inner = pl.ds(1, last)
    moves = (
        (own_ref.at[top, inner], out_ref.at[top, pl.ds(0, last)], (up, lon)),
        (own_ref.at[top, pl.ds(0, 1)], out_ref.at[top, pl.ds(last, 1)], (up, left)),
        (own_ref.at[bottom, pl.ds(0, 1)], out_ref.at[bottom, pl.ds(last, 1)], (lat, left)),
    )
    copies = [
        pltpu.make_async_remote_copy(
            src_ref=src, dst_ref=dst, send_sem=sends.at[i], recv_sem=recvs.at[i],
            device_id=who, device_id_type=MESH,
        )
        for i, (src, dst, who) in enumerate(moves)
    ]
    for copy in copies:
        copy.start()
    keep = pltpu.make_async_copy(
        own_ref.at[bottom, inner], out_ref.at[bottom, pl.ds(0, last)], local
    )
    keep.start()
    keep.wait()
    for copy in copies:
        copy.wait()


def attend_kernel(
    kinds_ref, joint_ref, gain_ref, wqkv_ref, wproj_ref, bias_ref,
    res_ref, pieces_ref,
    unit_ref, inv_ref, normed_ref, qkv_ref, dmix_ref, g_ref, mixed_ref, dqkv_ref,
    neg_ref, emb_ref, table_in, table_ref, grad_ref,
):
    lat = lax.axis_index("lat")
    lon = lax.axis_index("lon")
    nlat = lax.axis_size("lat")
    _, windows, wide, twice = joint_ref.shape
    channels = twice // 2
    tokens = WIN_LAT * wide
    head = channels // HEADS
    inv_sqrt = head ** (-0.5)
    total = WIN_LAT * windows * wide
    four = (WIN_LAT, windows, wide)

    x = joint_ref[:, :, :, :channels].reshape(total, channels).astype(f32)
    g = joint_ref[:, :, :, channels:].reshape(total, channels)
    g_ref[...] = g
    centre = x - jnp.mean(x, axis=-1, keepdims=True)
    inverse = lax.rsqrt(jnp.mean(centre * centre, axis=-1, keepdims=True) + norm_eps)
    unit = centre * inverse
    unit_ref[...] = unit
    inv_ref[...] = inverse
    normed = (unit * gain_ref[...]).astype(bf16)
    normed_ref[...] = normed
    qkv_ref[...] = nn(normed, wqkv_ref[...]).astype(bf16).reshape(four + (3 * channels,))
    dmix_ref[...] = nt(g, wproj_ref[...]).astype(bf16).reshape(four + (channels,))

    def place(index):
        slot = index >> 4
        row = jnp.where(slot >= HALF_LAT, slot - HALF_LAT, slot + HALF_LAT)
        side = (index >> 3) & 1
        column = index & 7
        return row, column, SPAN * row + HALF_LON * side + column

    row_i, _, _ = place(lax.broadcasted_iota(jnp.int32, (tokens, 128), 0))
    lane = TOP - lax.broadcasted_iota(jnp.int32, (tokens, 128), 1)
    good = lane > TOP
    for row in range(WIN_LAT):
        start = SPAN * row
        fits = (lane >= start) & (lane < start + WIN_LON)
        same = (row_i < HALF_LAT) if row < HALF_LAT else (row_i >= HALF_LAT)
        good = good | (fits & (same | (lat < nlat - 1)))
    neg_ref[...] = jnp.where(good, 0.0, masked_score)
    slot_j, column_j, place_j = place(lax.broadcasted_iota(jnp.int32, (128, tokens), 1))
    spot = TOP - lax.broadcasted_iota(jnp.int32, (128, tokens), 0)
    emb_ref[...] = jnp.where((spot == place_j) & (column_j < HALF_LON), 1.0, 0.0).astype(bf16)

    table_in[...] = jnp.zeros_like(table_in)
    table_in[:, :, : bias_ref.shape[2]] = bias_ref[...]
    table_ref[...] = jnp.zeros_like(table_ref)

    lane8 = lax.broadcasted_iota(jnp.int32, (PAD, 128), 1)
    sub8 = lax.broadcasted_iota(jnp.int32, (PAD, 256), 0)
    head_of = lax.broadcasted_iota(jnp.int32, (1, channels), 1) // head
    masks = [(head_of == h).astype(bf16) for h in range(HEADS)]
    masks32 = [(head_of == h).astype(f32) for h in range(HEADS)]
    bases = []
    for block in range(tokens // PAD):
        slot, side = block // 2, block % 2
        bases.append(SPAN * ((slot + HALF_LAT) % WIN_LAT) + HALF_LON * side)

    @pl.loop(0, windows)
    def _(w):
        kind = kinds_ref[lat, lon * windows + w]
        qkv = qkv_ref[:, w].reshape(tokens, 3 * channels)
        queries = qkv[:, :channels]
        emb = emb_ref[...]
        kv = nn(emb, qkv[:, channels:]).astype(bf16)
        keys, values = kv[:, :channels], kv[:, channels:]
        dmix = dmix_ref[:, w].reshape(tokens, channels)
        q_all = jnp.concatenate([queries * m for m in masks], axis=0)
        d_all = jnp.concatenate([dmix * m for m in masks], axis=0)
        raw = nt(q_all, keys)
        rows = table_in[kind]
        parts = []
        for h in range(HEADS):
            base = jnp.broadcast_to(rows[h : h + 1], (PAD, 256))
            for bit in (1, 2, 4):
                base = jnp.where((sub8 & bit) != 0, pltpu.roll(base, 256 - bit, 1), base)
            low, high = base[:, :128], base[:, 128:]
            for shift in bases:
                if shift == 0:
                    parts.append(low)
                else:
                    parts.append(
                        jnp.where(
                            lane8 < 128 - shift,
                            pltpu.roll(low, 128 - shift, 1),
                            pltpu.roll(high, 128 - shift, 1),
                        )
                    )
        bias = jnp.concatenate(parts, axis=0)
        neg = neg_ref[...]
        scores = raw * inv_sqrt + bias + jnp.concatenate([neg] * HEADS, axis=0)
        expo = jnp.exp(scores - jnp.max(scores, axis=-1, keepdims=True))
        probs = expo * (1.0 / jnp.sum(expo, axis=-1, keepdims=True))
        low_p = probs.astype(bf16)

        def fold(stacked):
            out = stacked[:tokens] * masks32[0]
            for h in range(1, HEADS):
                out = out + stacked[h * tokens : (h + 1) * tokens] * masks32[h]
            return out

        mixed_ref[:, w] = fold(nn(low_p, values)).astype(bf16).reshape(WIN_LAT, wide, channels)
        d_probs = nt(d_all, values)
        d_scores = probs * (d_probs - jnp.sum(probs * d_probs, axis=-1, keepdims=True))
        low_d = d_scores.astype(bf16)
        d_q = (fold(nn(low_d, keys)) * inv_sqrt).astype(bf16)
        d_k = (tn(low_d, q_all) * inv_sqrt).astype(bf16)
        d_v = tn(low_p, d_all).astype(bf16)
        d_kv = tn(emb, jnp.concatenate([d_k, d_v], axis=1)).astype(bf16)
        dqkv_ref[:, w] = jnp.concatenate([d_q, d_kv], axis=1).reshape(WIN_LAT, wide, 3 * channels)
        for h in range(HEADS):
            low = jnp.zeros((PAD, 128), f32)
            high = jnp.zeros((PAD, 128), f32)
            for block, shift in enumerate(bases):
                at = h * tokens + block * PAD
                tile = d_scores[at : at + PAD]
                if shift == 0:
                    low = low + tile
                else:
                    turned = pltpu.roll(tile, shift, 1)
                    low = low + jnp.where(lane8 >= shift, turned, 0.0)
                    high = high + jnp.where(lane8 < shift, turned, 0.0)
            table_ref[kind, h] += jnp.concatenate([low, high], axis=1)

    mixed = mixed_ref[...].reshape(total, channels)
    d_qkv = dqkv_ref[...].reshape(total, 3 * channels)
    branch = nn(mixed, wproj_ref[...])
    d_normed = nt(d_qkv, wqkv_ref[...])
    unit = unit_ref[...]
    grad_ref[:, : 3 * channels] = tn(normed_ref[...], d_qkv)
    grad_ref[:, 3 * channels :] = tn(mixed, g_ref[...])
    gain_grad = jnp.sum(d_normed * unit, axis=0, keepdims=True)
    d_unit = d_normed * gain_ref[...]
    path = inv_ref[...] * (
        d_unit
        - jnp.mean(d_unit, axis=-1, keepdims=True)
        - unit * jnp.mean(d_unit * unit, axis=-1, keepdims=True)
    )
    res_ref[:, :, :, :channels] = branch.astype(bf16).reshape(four + (channels,))
    res_ref[:, :, :, channels:] = path.astype(bf16).reshape(four + (channels,))

    table = table_ref[...]
    sub = lax.broadcasted_iota(jnp.int32, table.shape, 2)
    flat = table.reshape(-1, 256)
    sub = sub.reshape(-1, 256)
    for bit in (1, 2, 4):
        flat = jnp.where((sub & bit) != 0, pltpu.roll(flat, bit, 1), flat)
    binned = jnp.sum(flat.reshape(table.shape[0] * HEADS, PAD, 256), axis=1)

    pieces_ref[...] = jnp.zeros_like(pieces_ref)
    count = 0
    for column in range(4 * channels // 128):
        part = grad_ref[:, column * 128 : (column + 1) * 128].astype(bf16)
        pieces_ref[count : count + channels // 16] = part.reshape(channels // 16, 16, 128)
        count += channels // 16
    rows_t = binned.shape[0] // 16
    for side in range(2):
        part = binned[:, side * 128 : (side + 1) * 128].astype(bf16)
        pieces_ref[count : count + rows_t] = part.reshape(rows_t, 16, 128)
        count += rows_t
    gain_low = gain_grad.astype(bf16)
    pieces_ref[count, 0:1, :] = gain_low[:, :128]
    pieces_ref[count, 1:2, : channels - 128] = gain_low[:, 128:]


def finish_kernel(
    nlat, nlon, res_ref, own_ref, pieces_ref,
    both_ref, qkv_ref, proj_ref, table_ref, gain_ref,
    land_ref, rs_ref, red_ref, ag_ref, grad_ref,
    sends, recvs, rs_send, rs_recv, ag_send, ag_recv,
):
    lat = lax.axis_index("lat")
    lon = lax.axis_index("lon")
    count = nlat * nlon
    me = lat * nlon + lon
    share = red_ref.shape[0]
    last = own_ref.shape[1] - 1
    down, right = lax.rem(lat + 1, nlat), lax.rem(lon + 1, nlon)

    def peer(step):
        who = lax.rem(me + step, count)
        return who, (lax.div(who, nlon), lax.rem(who, nlon))

    barrier = pltpu.get_barrier_semaphore()

    @pl.loop(1, count)
    def _(step):
        pl.semaphore_signal(barrier, inc=1, device_id=peer(step)[1], device_id_type=MESH)

    pl.semaphore_wait(barrier, count - 1)

    def scatter(step):
        who, where = peer(step)
        return pltpu.make_async_remote_copy(
            src_ref=pieces_ref.at[pl.ds(who * share, share)],
            dst_ref=rs_ref.at[pl.ds((step - 1) * share, share)],
            send_sem=rs_send, recv_sem=rs_recv, device_id=where, device_id_type=MESH,
        )

    @pl.loop(1, count)
    def _(step):
        scatter(step).start()

    top = pl.ds(0, HALF_LAT)
    bottom = pl.ds(HALF_LAT, HALF_LAT)
    moves = (
        (res_ref.at[top, pl.ds(0, last)], land_ref.at[top, pl.ds(1, last)], (down, lon)),
        (res_ref.at[top, pl.ds(last, 1)], land_ref.at[top, pl.ds(0, 1)], (down, right)),
        (res_ref.at[bottom, pl.ds(last, 1)], land_ref.at[bottom, pl.ds(0, 1)], (lat, right)),
    )
    copies = [
        pltpu.make_async_remote_copy(
            src_ref=src, dst_ref=dst, send_sem=sends.at[i], recv_sem=recvs.at[i],
            device_id=who, device_id_type=MESH,
        )
        for i, (src, dst, who) in enumerate(moves)
    ]
    for copy in copies:
        copy.start()

    pltpu.make_async_copy(rs_ref, rs_ref, rs_recv).wait()
    summed = pieces_ref[pl.ds(me * share, share)].astype(f32)

    def add(step, running):
        return running + rs_ref[pl.ds(step * share, share)].astype(f32)

    summed = lax.fori_loop(0, count - 1, add, summed)
    red_ref[...] = summed.astype(bf16)

    def gather(step):
        return pltpu.make_async_remote_copy(
            src_ref=red_ref, dst_ref=ag_ref.at[pl.ds(me * share, share)],
            send_sem=ag_send, recv_sem=ag_recv, device_id=peer(step)[1], device_id_type=MESH,
        )

    @pl.loop(1, count)
    def _(step):
        gather(step).start()

    ag_ref[pl.ds(me * share, share)] = summed.astype(bf16)

    own_part = own_ref[bottom, 1:].astype(f32) + res_ref[bottom, :last].astype(f32)
    both_ref[bottom, 1:] = own_part.astype(bf16)
    for copy in copies:
        copy.wait()
    both_ref[top] = (own_ref[top].astype(f32) + land_ref[top].astype(f32)).astype(bf16)
    both_ref[bottom, 0:1] = (
        own_ref[bottom, 0:1].astype(f32) + land_ref[bottom, 0:1].astype(f32)
    ).astype(bf16)

    pltpu.make_async_copy(rs_ref, rs_ref, ag_recv).wait()
    channels = gain_ref.shape[1]
    at = 0
    for column in range(4 * channels // 128):
        part = ag_ref[at : at + channels // 16].astype(f32)
        grad_ref[:, column * 128 : (column + 1) * 128] = part.reshape(channels, 128)
        at += channels // 16
    kinds, heads, extent = table_ref.shape
    rows_t = kinds * heads // 16
    sides = []
    for side in range(2):
        sides.append(ag_ref[at : at + rows_t].astype(f32).reshape(kinds * heads, 128))
        at += rows_t
    table = jnp.concatenate(sides, axis=1)
    gain_block = ag_ref[at].astype(f32)
    gain = jnp.concatenate([gain_block[0:1], gain_block[1:2, : channels - 128]], axis=1)

    def scale(value, entries):
        mean = jnp.sum(jnp.sum(value * value, axis=1, keepdims=True), axis=0, keepdims=True)
        return jnp.minimum(1.0, lax.rsqrt(mean * (1.0 / entries) + clip_eps))

    wide = grad_ref[:, : 3 * channels]
    qkv_ref[...] = wide * scale(wide, wide.size)
    proj = grad_ref[:, 3 * channels :]
    proj_ref[...] = proj * scale(proj, proj.size)
    lane = lax.broadcasted_iota(jnp.int32, table.shape, 1)
    table = jnp.where(lane < extent, table, 0.0)
    table = table * scale(table, kinds * heads * extent)
    for kind in range(kinds):
        table_ref[kind] = table[kind * heads : (kind + 1) * heads, :extent]
    gain_ref[...] = gain * scale(gain, channels)

    pltpu.make_async_copy(rs_ref, rs_ref, rs_send).wait()
    pltpu.make_async_copy(rs_ref, rs_ref, ag_send).wait()


def on_device(nlat, nlon, state_grid, norm_gain, w_qkv, w_proj, bias_table, window_kind, cotangent):
    rows_dev, cols_dev, channels = state_grid.shape
    halves = cols_dev // HALF_LON
    windows = cols_dev // WIN_LON
    kinds, heads, extent = bias_table.shape
    devices = nlat * nlon
    joint = jnp.concatenate([state_grid, cotangent], axis=2)
    joint = joint.reshape(rows_dev, halves, HALF_LON, 2 * channels)
    joint = jnp.pad(joint, ((0, 0), (0, 0), (0, PAD - HALF_LON), (0, 0)))
    grid_shape = joint.shape

    block = pl.pallas_call(
        functools.partial(halo_kernel, nlat, nlon),
        name="halo",
        out_shape=jax.ShapeDtypeStruct(grid_shape, bf16),
        in_specs=[VM],
        out_specs=VM,
        scratch_shapes=[
            pltpu.SemaphoreType.DMA((3,)),
            pltpu.SemaphoreType.DMA((3,)),
            pltpu.SemaphoreType.DMA(()),
        ],
        compiler_params=pltpu.CompilerParams(collective_id=0, has_side_effects=True),
    )(joint)

    wide = 2 * PAD
    four = (WIN_LAT, windows, wide)
    total = WIN_LAT * windows * wide
    tokens = WIN_LAT * wide
    used = 4 * channels // 128 * (channels // 16) + 2 * (kinds * heads // 16) + 1
    share = -(-used // devices)
    res, pieces = pl.pallas_call(
        attend_kernel,
        name="attend",
        out_shape=(
            jax.ShapeDtypeStruct(four + (2 * channels,), bf16),
            jax.ShapeDtypeStruct((share * devices, 16, 128), bf16),
        ),
        in_specs=[pl.BlockSpec(memory_space=pltpu.SMEM)] + [VM] * 5,
        out_specs=(VM, VM),
        scratch_shapes=[
            pltpu.VMEM((total, channels), f32),
            pltpu.VMEM((total, 1), f32),
            pltpu.VMEM((total, channels), bf16),
            pltpu.VMEM(four + (3 * channels,), bf16),
            pltpu.VMEM(four + (channels,), bf16),
            pltpu.VMEM((total, channels), bf16),
            pltpu.VMEM(four + (channels,), bf16),
            pltpu.VMEM(four + (3 * channels,), bf16),
            pltpu.VMEM((tokens, 128), f32),
            pltpu.VMEM((128, tokens), bf16),
            pltpu.VMEM((kinds, heads, 256), f32),
            pltpu.VMEM((kinds, heads, PAD, 256), f32),
            pltpu.VMEM((channels, 4 * channels), f32),
        ],
    )(
        window_kind,
        block.reshape(four + (2 * channels,)),
        norm_gain.reshape(1, channels),
        w_qkv,
        w_proj,
        bias_table,
    )

    both, qkv_grad, proj_grad, table_grad, gain_grad = pl.pallas_call(
        functools.partial(finish_kernel, nlat, nlon),
        name="finish",
        out_shape=(
            jax.ShapeDtypeStruct(grid_shape, bf16),
            jax.ShapeDtypeStruct((channels, 3 * channels), f32),
            jax.ShapeDtypeStruct((channels, channels), f32),
            jax.ShapeDtypeStruct((kinds, heads, extent), f32),
            jax.ShapeDtypeStruct((1, channels), f32),
        ),
        in_specs=[VM] * 3,
        out_specs=(VM,) * 5,
        scratch_shapes=[
            pltpu.VMEM(grid_shape, bf16),
            pltpu.VMEM((share * (devices - 1), 16, 128), bf16),
            pltpu.VMEM((share, 16, 128), bf16),
            pltpu.VMEM((share * devices, 16, 128), bf16),
            pltpu.VMEM((channels, 4 * channels), f32),
            pltpu.SemaphoreType.DMA((3,)),
            pltpu.SemaphoreType.DMA((3,)),
            pltpu.SemaphoreType.DMA(()),
            pltpu.SemaphoreType.DMA(()),
            pltpu.SemaphoreType.DMA(()),
            pltpu.SemaphoreType.DMA(()),
        ],
        compiler_params=pltpu.CompilerParams(collective_id=1, has_side_effects=True),
    )(res.reshape(grid_shape), joint, pieces)

    both = both[:, :, :HALF_LON].reshape(rows_dev, cols_dev, 2 * channels)
    return (
        both[:, :, :channels],
        both[:, :, channels:],
        qkv_grad,
        proj_grad,
        table_grad,
        gain_grad.reshape(channels),
    )


def solution(mesh):
    in_specs = (P("lat", "lon", None), P(), P(), P(), P(), P(), P("lat", "lon", None))
    out_specs = (P("lat", "lon", None), P("lat", "lon", None), P(), P(), P(), P())
    body = functools.partial(on_device, mesh.shape["lat"], mesh.shape["lon"])
    return jax.shard_map(body, mesh=mesh, in_specs=in_specs, out_specs=out_specs, check_vma=False)
```

time: 260 us -> 75.5 us (0.29)
  waiting for transfers between devices: 127 us -> 0 us
  Pallas kernels: 0 us -> 65.4 us
  blocking collectives: 37.5 us -> 0 us
  matrix products: 25 us -> 0 us
  local copies, waits for them, and re-layouts: 26 us -> 7.79 us
  between operations: 17.3 us -> 0.68 us
  other arithmetic: 16.6 us -> 1.19 us
  starting transfers between devices: 9.66 us -> 0 us
    psum x1 -> x0, waiting for transfers between devices: 117 us -> none  [on_device(): lax.psum((grad_qkv, grad_proj, grad_table, grad_gain), ('lat', 'lon'))]
    pallas_call x0 -> x3, Pallas kernels: none -> 65.4 us  [the longest x1 33.1 us: on_device(): pl.pallas_call(functools.partial(finish_kernel, nlat, nlon), name='finish...]
    psum x1 -> x0, blocking collectives: 37.5 us -> none  [on_device(): lax.psum((grad_qkv, grad_proj, grad_table, grad_gain), ('lat', 'lon'))]
    dot_general x16 -> x0, matrix products: 25 us -> none  [the longest x1 2.81 us: window_bias(): jnp.dot(kind_onehot, spread.reshape(kind_count, heads_n * positions * pos...]
    ppermute x4 -> x0, waiting for transfers between devices: 9.65 us -> none  [shifted(): return lax.ppermute(value, axis, pairs)]
    ppermute x4 -> x0, starting transfers between devices: 9.62 us -> none  [shifted(): return lax.ppermute(value, axis, pairs)]
    reshape x10 -> x2, local copies, waits for them, and re-layouts: 8.95 us -> 1.33 us  [the longest x1 1.2 us: on_device(): both = both[:, :, :HALF_LON].reshape(rows_dev, cols_dev, 2 * channels)]
    reduce_sum x6 -> x0, other arithmetic: 5.09 us -> none  [the longest x4 4.62 us: clip_rms(): jnp.mean(gradient * gradient) + clip_eps]
  transfers between devices with their start and end apart: 5 -> 0, of which waited for: 4 -> 0; matrix products, arithmetic and copies ran while one was open for 6% -> 0% of each run, Pallas kernels for 0% -> 0%
where the time goes in v1:
time: 75.5 us; the launch traced here: 75.1 us
  Pallas kernels  65.4 us (87%)
  local copies, waits for them, and re-layouts  7.79 us (10%)
  other arithmetic  1.19 us (2%)
    pallas_call x1, Pallas kernels, on_device(): pl.pallas_call(functools.partial(finish_kernel, nlat, nlon), name='finish...  33.1 us
    pallas_call x1, Pallas kernels, on_device(): pl.pallas_call(attend_kernel, name='attend', out_shape=(jax.ShapeDtypeStr...  19.3 us
    pallas_call x1, Pallas kernels, on_device(): pl.pallas_call(functools.partial(halo_kernel, nlat, nlon), name='halo', o...  13 us
    unnamed x13, local copies, waits for them, and re-layouts  4.71 us

profile of v1, /device:TPU:0, one launch (start us, length us, event | category | flops | bytes accessed | tf_op | source)
XLA Modules:
  0.0 75.1 jit_solution(6602022908572400557)
XLA Ops:
  0.6 1.4 %copy.15.bias_ref = f32[8,6,253]{2,1,0:T(8,128)} copy(f32[8,6,253]{2,0,1:T(8,128)} %param.11) | data formatting | bytes 97152 | tf_op args[4]
  2.1 1.2 %pad_maximum_fusion = bf16[6,84,384]{2,1,0:T(8,128)(2,1)S(1)} fusion(bf16[6,84,192]{2,1,0:T(8,128)(2,1)} %param.13, bf16[6,84,192]{2,1,0:T(8,128)(2,1)} %param.7), kind=kLoop, calls=%fused_computation | loop fusion | flops 774144 | bytes 774144 | tf_op jit(solution)/shard_map/concatenate | solution.py:374
  3.3 0.1 reshape.30
  3.4 0.9 %pad.4.own_ref = bf16[6,14,8,384]{3,2,1,0:T(8,128)(2,1)} pad(bf16[6,14,6,384]{3,2,1,0:T(8,128)(2,1)S(1)} %reshape.30, bf16[]{:T(256)} %constant.2.clone.1), padding=0_0x0_0x0_2x0_0 | pad | bytes 903170 | tf_op jit(solution)/shard_map/jit(_pad)/pad | solution.py:376
  4.3 13.0 %halo.1 = bf16[6,14,8,384]{3,2,1,0:T(8,128)(2,1)} custom-call(bf16[6,14,8,384]{3,2,1,0:T(8,128)(2,1)} %pad.4.own_ref), custom_call_target="tpu_custom_call" | custom-call | tf_op jit(solution)/shard_map/halo/pallas_call | solution.py:379
  17.3 19.3 %attend.1 = (bf16[6,7,16,384]{3,2,1,0:T(8,128)(2,1)}, bf16[96,16,128]{2,1,0:T(8,128)(2,1)}) custom-call(s32[4,56]{1,0:T(4,128)} %kinds_ref.1, bf16[6,7,16,384]{3,2,1,0:T(8,128)(2,1)} %bitcast.5, f32[1,192]{1,0:T(1,128)} %bitcast.9, bf16[192,576]{1,0:T(8,128)(2,1)} %wqkv_ref.1, bf16[192,192]{1,0:T(8,128)(2,1)} %wproj_ref.1, f32[8,6,253]{2,1,0:T(8,128)} %copy.15.bias_ref), custom_call_target="tpu_custom_call" | custom-call | tf_op jit(solution)/shard_map/attend/pallas_call | solution.py:399
  36.6 33.1 %finish.1 = (bf16[6,14,8,384]{3,2,1,0:T(8,128)(2,1)}, f32[192,576]{1,0:T(8,128)}, f32[192,192]{1,0:T(8,128)}, f32[8,6,253]{2,1,0:T(8,128)}, f32[1,192]{1,0:T(1,128)}) custom-call(bf16[6,14,8,384]{3,2,1,0:T(8,128)(2,1)} %bitcast.7, bf16[6,14,8,384]{3,2,1,0:T(8,128)(2,1)} %pad.4.own_ref, bf16[96,16,128]{2,1,0:T(8,128)(2,1)} %get-tuple-element.14.pieces_ref), custom_call_target="tpu_custom_call" | custom-call | tf_op jit(solution)/shard_map/finish/pallas_call | solution.py:432
  69.7 0.0 copy-start.2
  69.7 1.2 %reshape.34 = bf16[6,84,384]{2,1,0:T(8,128)(2,1)S(1)} reshape(bf16[6,14,6,384]{3,2,1,0:T(8,128)(2,1)} %bitcast.6) | data formatting | bytes 774144 | tf_op jit(solution)/shard_map/reshape | solution.py:460
  70.9 0.0 copy-done.2
  71.0 0.6 copy.16
  71.6 0.0 copy-start
  71.6 0.9 %fusion = (bf16[6,84,192]{2,1,0:T(8,128)(2,1)}, bf16[6,84,192]{2,1,0:T(8,128)(2,1)}) fusion(bf16[6,84,384]{2,1,0:T(8,128)(2,1)S(1)} %reshape.34), kind=kLoop, calls=%fused_computation.1 | loop fusion | bytes 774144 | tf_op jit(solution)/shard_map/slice | solution.py:463
  72.5 0.3 copy-done
  72.7 0.0 copy-start.1
  72.7 0.8 %copy.20 = f32[192,576]{1,0:T(8,128)} copy(f32[192,576]{1,0:T(8,128)S(1)} %copy-done) | data formatting | bytes 884736
  73.5 0.3 copy-done.1
  73.9 0.0 copy-start.3
  73.9 0.7 copy.21
  74.5 0.0 copy-done.3
  74.5 0.6 copy.22
Async XLA Ops:
  69.7 1.2 %copy-start.2 = (f32[8,6,253]{2,1,0:T(8,128)S(1)}, f32[8,6,253]{2,1,0:T(8,128)}, u32[]{:S(2)}) copy-start(f32[8,6,253]{2,1,0:T(8,128)} %get-tuple-element.30) | copy-start | bytes 145732
  71.6 1.1 %copy-start = (f32[192,576]{1,0:T(8,128)S(1)}, f32[192,576]{1,0:T(8,128)}, u32[]{:S(2)}) copy-start(f32[192,576]{1,0:T(8,128)} %get-tuple-element.42) | copy-start | bytes 1327108
  72.7 1.1 %copy-start.1 = (f32[192,192]{1,0:T(8,128)S(1)}, f32[192,192]{1,0:T(8,128)}, u32[]{:S(2)}) copy-start(f32[192,192]{1,0:T(8,128)} %get-tuple-element.43) | copy-start | bytes 442372
  73.9 0.7 copy-start.3

commit v2 on v1

--- a/solution.py
+++ b/solution.py
@@ -13,6 +13,7 @@
 HALF_LAT = 3
 HALF_LON = 6
 PAD = 8
+ROWS = 8
 SPAN = 2 * WIN_LON - 1
 TOP = (WIN_LAT - 1) * SPAN + WIN_LON - 1
 
@@ -232,12 +233,12 @@
     count = 0
     for column in range(4 * channels // 128):
         part = grad_ref[:, column * 128 : (column + 1) * 128].astype(bf16)
-        pieces_ref[count : count + channels // 16] = part.reshape(channels // 16, 16, 128)
-        count += channels // 16
-    rows_t = binned.shape[0] // 16
+        pieces_ref[count : count + channels // ROWS] = part.reshape(channels // ROWS, ROWS, 128)
+        count += channels // ROWS
+    rows_t = binned.shape[0] // ROWS
     for side in range(2):
         part = binned[:, side * 128 : (side + 1) * 128].astype(bf16)
-        pieces_ref[count : count + rows_t] = part.reshape(rows_t, 16, 128)
+        pieces_ref[count : count + rows_t] = part.reshape(rows_t, ROWS, 128)
         count += rows_t
     gain_low = gain_grad.astype(bf16)
     pieces_ref[count, 0:1, :] = gain_low[:, :128]
@@ -247,40 +248,46 @@
 def finish_kernel(
     nlat, nlon, res_ref, own_ref, pieces_ref,
     both_ref, qkv_ref, proj_ref, table_ref, gain_ref,
-    land_ref, rs_ref, red_ref, ag_ref, grad_ref,
-    sends, recvs, rs_send, rs_recv, ag_send, ag_recv,
+    land_ref, rs1_ref, mid_ref, rs2_ref, ag2_ref, ag_ref, grad_ref,
+    sends, recvs, lon_send, lon_recv, lat_send, lat_recv,
 ):
     lat = lax.axis_index("lat")
     lon = lax.axis_index("lon")
-    count = nlat * nlon
-    me = lat * nlon + lon
-    share = red_ref.shape[0]
+    chunk = mid_ref.shape[0]
+    share = chunk // nlat
     last = own_ref.shape[1] - 1
     down, right = lax.rem(lat + 1, nlat), lax.rem(lon + 1, nlon)
-
-    def peer(step):
-        who = lax.rem(me + step, count)
-        return who, (lax.div(who, nlon), lax.rem(who, nlon))
+    up, left = lax.rem(lat + nlat - 1, nlat), lax.rem(lon + nlon - 1, nlon)
 
     barrier = pltpu.get_barrier_semaphore()
-
-    @pl.loop(1, count)
+    for step in range(1, nlon):
+        who = (lat, lax.rem(lon + step, nlon))
+        pl.semaphore_signal(barrier, inc=1, device_id=who, device_id_type=MESH)
+    for step in range(1, nlat):
+        who = (lax.rem(lat + step, nlat), lon)
+        pl.semaphore_signal(barrier, inc=1, device_id=who, device_id_type=MESH)
+    pl.semaphore_signal(barrier, inc=1, device_id=(up, left), device_id_type=MESH)
+    pl.semaphore_wait(barrier, nlon + nlat - 1)
+
+    def along_lon(src, dst, which, step):
+        return pltpu.make_async_remote_copy(
+            src_ref=src, dst_ref=dst, send_sem=lon_send.at[which], recv_sem=lon_recv.at[which],
+            device_id=(lat, lax.rem(lon + step, nlon)), device_id_type=MESH,
+        )
+
+    def along_lat(src, dst, which, step):
+        return pltpu.make_async_remote_copy(
+            src_ref=src, dst_ref=dst, send_sem=lat_send.at[which], recv_sem=lat_recv.at[which],
+            device_id=(lax.rem(lat + step, nlat), lon), device_id_type=MESH,
+        )
+
+    @pl.loop(1, nlon)
     def _(step):
-        pl.semaphore_signal(barrier, inc=1, device_id=peer(step)[1], device_id_type=MESH)
-
-    pl.semaphore_wait(barrier, count - 1)
-
-    def scatter(step):
-        who, where = peer(step)
-        return pltpu.make_async_remote_copy(
-            src_ref=pieces_ref.at[pl.ds(who * share, share)],
-            dst_ref=rs_ref.at[pl.ds((step - 1) * share, share)],
-            send_sem=rs_send, recv_sem=rs_recv, device_id=where, device_id_type=MESH,
-        )
-
-    @pl.loop(1, count)
-    def _(step):
-        scatter(step).start()
+        who = lax.rem(lon + step, nlon)
+        along_lon(
+            pieces_ref.at[pl.ds(who * chunk, chunk)],
+            rs1_ref.at[pl.ds((step - 1) * chunk, chunk)], 0, step,
+        ).start()
 
     top = pl.ds(0, HALF_LAT)
     bottom = pl.ds(HALF_LAT, HALF_LAT)
@@ -299,29 +306,42 @@
     for copy in copies:
         copy.start()
 
-    pltpu.make_async_copy(rs_ref, rs_ref, rs_recv).wait()
-    summed = pieces_ref[pl.ds(me * share, share)].astype(f32)
-
-    def add(step, running):
-        return running + rs_ref[pl.ds(step * share, share)].astype(f32)
-
-    summed = lax.fori_loop(0, count - 1, add, summed)
-    red_ref[...] = summed.astype(bf16)
-
-    def gather(step):
-        return pltpu.make_async_remote_copy(
-            src_ref=red_ref, dst_ref=ag_ref.at[pl.ds(me * share, share)],
-            send_sem=ag_send, recv_sem=ag_recv, device_id=peer(step)[1], device_id_type=MESH,
-        )
-
-    @pl.loop(1, count)
-    def _(step):
-        gather(step).start()
-
-    ag_ref[pl.ds(me * share, share)] = summed.astype(bf16)
-
     own_part = own_ref[bottom, 1:].astype(f32) + res_ref[bottom, :last].astype(f32)
     both_ref[bottom, 1:] = own_part.astype(bf16)
+
+    pltpu.make_async_copy(rs1_ref, rs1_ref, lon_recv.at[0]).wait()
+    summed = pieces_ref[pl.ds(lon * chunk, chunk)].astype(f32)
+    for step in range(nlon - 1):
+        summed = summed + rs1_ref[step * chunk : (step + 1) * chunk].astype(f32)
+    mid_ref[...] = summed.astype(bf16)
+
+    @pl.loop(1, nlat)
+    def _(step):
+        who = lax.rem(lat + step, nlat)
+        along_lat(
+            mid_ref.at[pl.ds(who * share, share)],
+            rs2_ref.at[pl.ds((step - 1) * share, share)], 0, step,
+        ).start()
+
+    pltpu.make_async_copy(rs2_ref, rs2_ref, lat_recv.at[0]).wait()
+    total = mid_ref[pl.ds(lat * share, share)].astype(f32)
+    for step in range(nlat - 1):
+        total = total + rs2_ref[step * share : (step + 1) * share].astype(f32)
+    ag2_ref[pl.ds(lat * share, share)] = total.astype(bf16)
+
+    @pl.loop(1, nlat)
+    def _(step):
+        mine = ag2_ref.at[pl.ds(lat * share, share)]
+        along_lat(mine, mine, 1, step).start()
+
+    pltpu.make_async_copy(rs2_ref, rs2_ref, lat_recv.at[1]).wait()
+
+    @pl.loop(1, nlon)
+    def _(step):
+        along_lon(ag2_ref, ag_ref.at[pl.ds(lon * chunk, chunk)], 1, step).start()
+
+    ag_ref[pl.ds(lon * chunk, chunk)] = ag2_ref[...]
+
     for copy in copies:
         copy.wait()
     both_ref[top] = (own_ref[top].astype(f32) + land_ref[top].astype(f32)).astype(bf16)
@@ -329,15 +349,15 @@
         own_ref[bottom, 0:1].astype(f32) + land_ref[bottom, 0:1].astype(f32)
     ).astype(bf16)
 
-    pltpu.make_async_copy(rs_ref, rs_ref, ag_recv).wait()
+    pltpu.make_async_copy(rs1_ref, rs1_ref, lon_recv.at[1]).wait()
     channels = gain_ref.shape[1]
     at = 0
     for column in range(4 * channels // 128):
-        part = ag_ref[at : at + channels // 16].astype(f32)
+        part = ag_ref[at : at + channels // ROWS].astype(f32)
         grad_ref[:, column * 128 : (column + 1) * 128] = part.reshape(channels, 128)
-        at += channels // 16
+        at += channels // ROWS
     kinds, heads, extent = table_ref.shape
-    rows_t = kinds * heads // 16
+    rows_t = kinds * heads // ROWS
     sides = []
     for side in range(2):
         sides.append(ag_ref[at : at + rows_t].astype(f32).reshape(kinds * heads, 128))
@@ -361,8 +381,9 @@
         table_ref[kind] = table[kind * heads : (kind + 1) * heads, :extent]
     gain_ref[...] = gain * scale(gain, channels)
 
-    pltpu.make_async_copy(rs_ref, rs_ref, rs_send).wait()
-    pltpu.make_async_copy(rs_ref, rs_ref, ag_send).wait()
+    for which in range(2):
+        pltpu.make_async_copy(rs1_ref, rs1_ref, lon_send.at[which]).wait()
+        pltpu.make_async_copy(rs2_ref, rs2_ref, lat_send.at[which]).wait()
 
 
 def on_device(nlat, nlon, state_grid, norm_gain, w_qkv, w_proj, bias_table, window_kind, cotangent):
@@ -394,14 +415,14 @@
     four = (WIN_LAT, windows, wide)
     total = WIN_LAT * windows * wide
     tokens = WIN_LAT * wide
-    used = 4 * channels // 128 * (channels // 16) + 2 * (kinds * heads // 16) + 1
+    used = 4 * channels // 128 * (channels // ROWS) + 2 * (kinds * heads // ROWS) + 1
     share = -(-used // devices)
     res, pieces = pl.pallas_call(
         attend_kernel,
         name="attend",
         out_shape=(
             jax.ShapeDtypeStruct(four + (2 * channels,), bf16),
-            jax.ShapeDtypeStruct((share * devices, 16, 128), bf16),
+            jax.ShapeDtypeStruct((share * devices, ROWS, 128), bf16),
         ),
         in_specs=[pl.BlockSpec(memory_space=pltpu.SMEM)] + [VM] * 5,
         out_specs=(VM, VM),
@@ -443,16 +464,18 @@
         out_specs=(VM,) * 5,
         scratch_shapes=[
             pltpu.VMEM(grid_shape, bf16),
-            pltpu.VMEM((share * (devices - 1), 16, 128), bf16),
-            pltpu.VMEM((share, 16, 128), bf16),
-            pltpu.VMEM((share * devices, 16, 128), bf16),
+            pltpu.VMEM((share * nlat * (nlon - 1), ROWS, 128), bf16),
+            pltpu.VMEM((share * nlat, ROWS, 128), bf16),
+            pltpu.VMEM((share * (nlat - 1), ROWS, 128), bf16),
+            pltpu.VMEM((share * nlat, ROWS, 128), bf16),
+            pltpu.VMEM((share * devices, ROWS, 128), bf16),
             pltpu.VMEM((channels, 4 * channels), f32),
             pltpu.SemaphoreType.DMA((3,)),
             pltpu.SemaphoreType.DMA((3,)),
-            pltpu.SemaphoreType.DMA(()),
-            pltpu.SemaphoreType.DMA(()),
-            pltpu.SemaphoreType.DMA(()),
-            pltpu.SemaphoreType.DMA(()),
+            pltpu.SemaphoreType.DMA((2,)),
+            pltpu.SemaphoreType.DMA((2,)),
+            pltpu.SemaphoreType.DMA((2,)),
+            pltpu.SemaphoreType.DMA((2,)),
         ],
         compiler_params=pltpu.CompilerParams(collective_id=1, has_side_effects=True),
     )(res.reshape(grid_shape), joint, pieces)

time: 75.5 us -> 67.1 us (0.89)
  Pallas kernels: 65.4 us -> 57 us
    pallas_call x1, Pallas kernels: 33.1 us -> 24.7 us  [on_device(): pl.pallas_call(functools.partial(finish_kernel, nlat, nlon), name='finish...]
where the time goes in v2:
time: 67.1 us; the launch traced here: 66.7 us
  Pallas kernels  57 us (85%)
  local copies, waits for them, and re-layouts  7.79 us (12%)
  other arithmetic  1.19 us (2%)
  between operations  0.68 us (1%)
    pallas_call x1, Pallas kernels, on_device(): pl.pallas_call(functools.partial(finish_kernel, nlat, nlon), name='finish...  24.7 us
    pallas_call x1, Pallas kernels, on_device(): pl.pallas_call(attend_kernel, name='attend', out_shape=(jax.ShapeDtypeStr...  19.3 us
    pallas_call x1, Pallas kernels, on_device(): pl.pallas_call(functools.partial(halo_kernel, nlat, nlon), name='halo', o...  13 us
    unnamed x13, local copies, waits for them, and re-layouts  4.71 us

profile of v2, /device:TPU:0, one launch (start us, length us, event | category | flops | bytes accessed | tf_op | source)
XLA Modules:
  0.0 66.7 jit_solution(15845569391804706960)
XLA Ops:
  0.6 1.4 %copy.15.bias_ref = f32[8,6,253]{2,1,0:T(8,128)} copy(f32[8,6,253]{2,0,1:T(8,128)} %param.11) | data formatting | bytes 97152 | tf_op args[4]
  2.1 1.2 %pad_maximum_fusion = bf16[6,84,384]{2,1,0:T(8,128)(2,1)S(1)} fusion(bf16[6,84,192]{2,1,0:T(8,128)(2,1)} %param.13, bf16[6,84,192]{2,1,0:T(8,128)(2,1)} %param.7), kind=kLoop, calls=%fused_computation | loop fusion | flops 774144 | bytes 774144 | tf_op jit(solution)/shard_map/concatenate | solution.py:395
  3.3 0.1 reshape.30
  3.4 0.9 %pad.4.own_ref = bf16[6,14,8,384]{3,2,1,0:T(8,128)(2,1)} pad(bf16[6,14,6,384]{3,2,1,0:T(8,128)(2,1)S(1)} %reshape.30, bf16[]{:T(256)} %constant.2.clone.1), padding=0_0x0_0x0_2x0_0 | pad | bytes 903170 | tf_op jit(solution)/shard_map/jit(_pad)/pad | solution.py:397
  4.3 13.0 %halo.1 = bf16[6,14,8,384]{3,2,1,0:T(8,128)(2,1)} custom-call(bf16[6,14,8,384]{3,2,1,0:T(8,128)(2,1)} %pad.4.own_ref), custom_call_target="tpu_custom_call" | custom-call | tf_op jit(solution)/shard_map/halo/pallas_call | solution.py:400
  17.3 19.3 %attend.1 = (bf16[6,7,16,384]{3,2,1,0:T(8,128)(2,1)}, bf16[160,8,128]{2,1,0:T(8,128)(2,1)}) custom-call(s32[4,56]{1,0:T(4,128)} %kinds_ref.1, bf16[6,7,16,384]{3,2,1,0:T(8,128)(2,1)} %bitcast.5, f32[1,192]{1,0:T(1,128)} %bitcast.9, bf16[192,576]{1,0:T(8,128)(2,1)} %wqkv_ref.1, bf16[192,192]{1,0:T(8,128)(2,1)} %wproj_ref.1, f32[8,6,253]{2,1,0:T(8,128)} %copy.15.bias_ref), custom_call_target="tpu_custom_call" | custom-call | tf_op jit(solution)/shard_map/attend/pallas_call | solution.py:420
  36.6 24.7 %finish.1 = (bf16[6,14,8,384]{3,2,1,0:T(8,128)(2,1)}, f32[192,576]{1,0:T(8,128)}, f32[192,192]{1,0:T(8,128)}, f32[8,6,253]{2,1,0:T(8,128)}, f32[1,192]{1,0:T(1,128)}) custom-call(bf16[6,14,8,384]{3,2,1,0:T(8,128)(2,1)} %bitcast.7, bf16[6,14,8,384]{3,2,1,0:T(8,128)(2,1)} %pad.4.own_ref, bf16[160,8,128]{2,1,0:T(8,128)(2,1)} %get-tuple-element.14.pieces_ref), custom_call_target="tpu_custom_call" | custom-call | tf_op jit(solution)/shard_map/finish/pallas_call | solution.py:453
  61.3 0.0 copy-start.2
  61.3 1.2 %reshape.34 = bf16[6,84,384]{2,1,0:T(8,128)(2,1)S(1)} reshape(bf16[6,14,6,384]{3,2,1,0:T(8,128)(2,1)} %bitcast.6) | data formatting | bytes 774144 | tf_op jit(solution)/shard_map/reshape | solution.py:483
  62.5 0.0 copy-done.2
  62.5 0.6 copy.16
  63.2 0.0 copy-start
  63.2 0.9 %fusion = (bf16[6,84,192]{2,1,0:T(8,128)(2,1)}, bf16[6,84,192]{2,1,0:T(8,128)(2,1)}) fusion(bf16[6,84,384]{2,1,0:T(8,128)(2,1)S(1)} %reshape.34), kind=kLoop, calls=%fused_computation.1 | loop fusion | bytes 774144 | tf_op jit(solution)/shard_map/slice | solution.py:486
  64.0 0.3 copy-done
  64.3 0.0 copy-start.1
  64.3 0.8 %copy.20 = f32[192,576]{1,0:T(8,128)} copy(f32[192,576]{1,0:T(8,128)S(1)} %copy-done) | data formatting | bytes 884736
  65.1 0.3 copy-done.1
  65.4 0.0 copy-start.3
  65.4 0.7 %copy.21 = f32[192,192]{1,0:T(8,128)} copy(f32[192,192]{1,0:T(8,128)S(1)} %copy-done.1) | data formatting | bytes 294912
  66.1 0.0 copy-done.3
  66.1 0.6 copy.22
Async XLA Ops:
  61.3 1.2 %copy-start.2 = (f32[8,6,253]{2,1,0:T(8,128)S(1)}, f32[8,6,253]{2,1,0:T(8,128)}, u32[]{:S(2)}) copy-start(f32[8,6,253]{2,1,0:T(8,128)} %get-tuple-element.30) | copy-start | bytes 145732
  63.2 1.1 %copy-start = (f32[192,576]{1,0:T(8,128)S(1)}, f32[192,576]{1,0:T(8,128)}, u32[]{:S(2)}) copy-start(f32[192,576]{1,0:T(8,128)} %get-tuple-element.42) | copy-start | bytes 1327108
  64.3 1.1 %copy-start.1 = (f32[192,192]{1,0:T(8,128)S(1)}, f32[192,192]{1,0:T(8,128)}, u32[]{:S(2)}) copy-start(f32[192,192]{1,0:T(8,128)} %get-tuple-element.43) | copy-start | bytes 442372
  65.4 0.7 %copy-start.3 = (f32[1,192]{1,0:T(1,128)S(1)}, f32[1,192]{1,0:T(1,128)}, u32[]{:S(2)}) copy-start(f32[1,192]{1,0:T(1,128)} %get-tuple-element.19) | copy-start | bytes 2308

commit v3 on v2

--- a/solution.py
+++ b/solution.py
@@ -38,71 +38,82 @@
     return jnp.dot(a, b, preferred_element_type=f32)
 
 
-def halo_kernel(nlat, nlon, own_ref, out_ref, sends, recvs, local):
-    lat = lax.axis_index("lat")
-    lon = lax.axis_index("lon")
-    last = own_ref.shape[1] - 1
-    up, down = lax.rem(lat + nlat - 1, nlat), lax.rem(lat + 1, nlat)
-    left, right = lax.rem(lon + nlon - 1, nlon), lax.rem(lon + 1, nlon)
-    barrier = pltpu.get_barrier_semaphore()
-    for who in ((down, lon), (lat, right), (down, right)):
-        pl.semaphore_signal(barrier, inc=1, device_id=who, device_id_type=MESH)
-    pl.semaphore_wait(barrier, 3)
-    top = pl.ds(0, HALF_LAT)
-    bottom = pl.ds(HALF_LAT, HALF_LAT)
-    inner = pl.ds(1, last)
-    moves = (
-        (own_ref.at[top, inner], out_ref.at[top, pl.ds(0, last)], (up, lon)),
-        (own_ref.at[top, pl.ds(0, 1)], out_ref.at[top, pl.ds(last, 1)], (up, left)),
-        (own_ref.at[bottom, pl.ds(0, 1)], out_ref.at[bottom, pl.ds(last, 1)], (lat, left)),
-    )
-    copies = [
-        pltpu.make_async_remote_copy(
-            src_ref=src, dst_ref=dst, send_sem=sends.at[i], recv_sem=recvs.at[i],
-            device_id=who, device_id_type=MESH,
-        )
-        for i, (src, dst, who) in enumerate(moves)
-    ]
-    for copy in copies:
-        copy.start()
-    keep = pltpu.make_async_copy(
-        own_ref.at[bottom, inner], out_ref.at[bottom, pl.ds(0, last)], local
-    )
-    keep.start()
-    keep.wait()
-    for copy in copies:
-        copy.wait()
-
-
-def attend_kernel(
-    kinds_ref, joint_ref, gain_ref, wqkv_ref, wproj_ref, bias_ref,
-    res_ref, pieces_ref,
+def block_kernel(
+    nlat, nlon, kinds_ref, own_ref, gain_ref, wqkv_ref, wproj_ref, bias_ref,
+    both_ref, qkv_out, proj_out, table_out, gain_out,
+    block_ref, res_ref, pieces_ref,
     unit_ref, inv_ref, normed_ref, qkv_ref, dmix_ref, g_ref, mixed_ref, dqkv_ref,
     neg_ref, emb_ref, table_in, table_ref, grad_ref,
+    land_ref, rs1_ref, mid_ref, rs2_ref, ag2_ref, ag_ref,
+    halo_send, halo_recv, local, sends, recvs, lon_send, lon_recv, lat_send, lat_recv,
 ):
     lat = lax.axis_index("lat")
     lon = lax.axis_index("lon")
-    nlat = lax.axis_size("lat")
-    _, windows, wide, twice = joint_ref.shape
+    _, halves, _, twice = own_ref.shape
     channels = twice // 2
+    windows = halves // 2
+    wide = 2 * PAD
+    last = halves - 1
     tokens = WIN_LAT * wide
     head = channels // HEADS
     inv_sqrt = head ** (-0.5)
     total = WIN_LAT * windows * wide
     four = (WIN_LAT, windows, wide)
-
-    x = joint_ref[:, :, :, :channels].reshape(total, channels).astype(f32)
-    g = joint_ref[:, :, :, channels:].reshape(total, channels)
-    g_ref[...] = g
-    centre = x - jnp.mean(x, axis=-1, keepdims=True)
-    inverse = lax.rsqrt(jnp.mean(centre * centre, axis=-1, keepdims=True) + norm_eps)
-    unit = centre * inverse
-    unit_ref[...] = unit
-    inv_ref[...] = inverse
-    normed = (unit * gain_ref[...]).astype(bf16)
-    normed_ref[...] = normed
-    qkv_ref[...] = nn(normed, wqkv_ref[...]).astype(bf16).reshape(four + (3 * channels,))
-    dmix_ref[...] = nt(g, wproj_ref[...]).astype(bf16).reshape(four + (channels,))
+    chunk = mid_ref.shape[0]
+    share = chunk // nlat
+    down, right = lax.rem(lat + 1, nlat), lax.rem(lon + 1, nlon)
+    up, left = lax.rem(lat + nlat - 1, nlat), lax.rem(lon + nlon - 1, nlon)
+
+    barrier = pltpu.get_barrier_semaphore()
+    for step in range(1, nlon):
+        who = (lat, lax.rem(lon + step, nlon))
+        pl.semaphore_signal(barrier, inc=1, device_id=who, device_id_type=MESH)
+    for step in range(1, nlat):
+        who = (lax.rem(lat + step, nlat), lon)
+        pl.semaphore_signal(barrier, inc=1, device_id=who, device_id_type=MESH)
+    for who in ((up, left), (down, right)):
+        pl.semaphore_signal(barrier, inc=1, device_id=who, device_id_type=MESH)
+    pl.semaphore_wait(barrier, nlon + nlat)
+
+    top = pl.ds(0, HALF_LAT)
+    bottom = pl.ds(HALF_LAT, HALF_LAT)
+    inner = pl.ds(1, last)
+    moves = (
+        (own_ref.at[bottom, pl.ds(0, 1)], block_ref.at[bottom, pl.ds(last, 1)], (lat, left)),
+        (own_ref.at[top, inner], block_ref.at[top, pl.ds(0, last)], (up, lon)),
+        (own_ref.at[top, pl.ds(0, 1)], block_ref.at[top, pl.ds(last, 1)], (up, left)),
+    )
+    fetch = [
+        pltpu.make_async_remote_copy(
+            src_ref=src, dst_ref=dst, send_sem=halo_send.at[i], recv_sem=halo_recv.at[i],
+            device_id=who, device_id_type=MESH,
+        )
+        for i, (src, dst, who) in enumerate(moves)
+    ]
+    for copy in fetch:
+        copy.start()
+    keep = pltpu.make_async_copy(
+        own_ref.at[bottom, inner], block_ref.at[bottom, pl.ds(0, last)], local
+    )
+    keep.start()
+
+    def prepare(first):
+        here = slice(first, first + HALF_LAT)
+        count = HALF_LAT * windows * wide
+        rows = slice(first * windows * wide, first * windows * wide + count)
+        three = (HALF_LAT, windows, wide)
+        x = block_ref[here, :, :, :channels].astype(f32).reshape(count, channels)
+        g = block_ref[here, :, :, channels:].astype(f32).reshape(count, channels).astype(bf16)
+        g_ref[rows] = g
+        centre = x - jnp.mean(x, axis=-1, keepdims=True)
+        inverse = lax.rsqrt(jnp.mean(centre * centre, axis=-1, keepdims=True) + norm_eps)
+        unit = centre * inverse
+        unit_ref[rows] = unit
+        inv_ref[rows] = inverse
+        normed = (unit * gain_ref[...]).astype(bf16)
+        normed_ref[rows] = normed
+        qkv_ref[here] = nn(normed, wqkv_ref[...]).astype(bf16).reshape(three + (3 * channels,))
+        dmix_ref[here] = nt(g, wproj_ref[...]).astype(bf16).reshape(three + (channels,))
 
     def place(index):
         slot = index >> 4
@@ -128,7 +139,15 @@
     table_in[:, :, : bias_ref.shape[2]] = bias_ref[...]
     table_ref[...] = jnp.zeros_like(table_ref)
 
+    keep.wait()
+    fetch[0].wait_recv()
+    prepare(HALF_LAT)
+    fetch[1].wait_recv()
+    fetch[2].wait_recv()
+    prepare(0)
+
     lane8 = lax.broadcasted_iota(jnp.int32, (PAD, 128), 1)
+    kind_of = lax.broadcasted_iota(jnp.int32, (bias_ref.shape[1], PAD, 256), 0)
     sub8 = lax.broadcasted_iota(jnp.int32, (PAD, 256), 0)
     head_of = lax.broadcasted_iota(jnp.int32, (1, channels), 1) // head
     masks = [(head_of == h).astype(bf16) for h in range(HEADS)]
@@ -150,10 +169,9 @@
         q_all = jnp.concatenate([queries * m for m in masks], axis=0)
         d_all = jnp.concatenate([dmix * m for m in masks], axis=0)
         raw = nt(q_all, keys)
-        rows = table_in[kind]
         parts = []
         for h in range(HEADS):
-            base = jnp.broadcast_to(rows[h : h + 1], (PAD, 256))
+            base = jnp.broadcast_to(table_in[h, pl.ds(kind, 1)], (PAD, 256))
             for bit in (1, 2, 4):
                 base = jnp.where((sub8 & bit) != 0, pltpu.roll(base, 256 - bit, 1), base)
             low, high = base[:, :128], base[:, 128:]
@@ -202,24 +220,40 @@
                     turned = pltpu.roll(tile, shift, 1)
                     low = low + jnp.where(lane8 >= shift, turned, 0.0)
                     high = high + jnp.where(lane8 < shift, turned, 0.0)
-            table_ref[kind, h] += jnp.concatenate([low, high], axis=1)
+            tile = jnp.concatenate([low, high], axis=1)
+            table_ref[h] += jnp.where(kind_of == kind, tile[None], 0.0)
 
     mixed = mixed_ref[...].reshape(total, channels)
     d_qkv = dqkv_ref[...].reshape(total, 3 * channels)
     branch = nn(mixed, wproj_ref[...])
     d_normed = nt(d_qkv, wqkv_ref[...])
     unit = unit_ref[...]
-    grad_ref[:, : 3 * channels] = tn(normed_ref[...], d_qkv)
-    grad_ref[:, 3 * channels :] = tn(mixed, g_ref[...])
-    gain_grad = jnp.sum(d_normed * unit, axis=0, keepdims=True)
     d_unit = d_normed * gain_ref[...]
     path = inv_ref[...] * (
         d_unit
         - jnp.mean(d_unit, axis=-1, keepdims=True)
         - unit * jnp.mean(d_unit * unit, axis=-1, keepdims=True)
     )
-    res_ref[:, :, :, :channels] = branch.astype(bf16).reshape(four + (channels,))
-    res_ref[:, :, :, channels:] = path.astype(bf16).reshape(four + (channels,))
+    grid = (WIN_LAT, halves, PAD, channels)
+    res_ref[:, :, :, :channels] = branch.reshape(grid).astype(bf16)
+    res_ref[:, :, :, channels:] = path.reshape(grid).astype(bf16)
+    gain_grad = jnp.sum(d_normed * unit, axis=0, keepdims=True)
+    moves = (
+        (res_ref.at[top, pl.ds(0, last)], land_ref.at[top, pl.ds(1, last)], (down, lon)),
+        (res_ref.at[top, pl.ds(last, 1)], land_ref.at[top, pl.ds(0, 1)], (down, right)),
+        (res_ref.at[bottom, pl.ds(last, 1)], land_ref.at[bottom, pl.ds(0, 1)], (lat, right)),
+    )
+    copies = [
+        pltpu.make_async_remote_copy(
+            src_ref=src, dst_ref=dst, send_sem=sends.at[i], recv_sem=recvs.at[i],
+            device_id=who, device_id_type=MESH,
+        )
+        for i, (src, dst, who) in enumerate(moves)
+    ]
+    for copy in copies:
+        copy.start()
+    grad_ref[:, : 3 * channels] = tn(normed_ref[...], d_qkv)
+    grad_ref[:, 3 * channels :] = tn(mixed, g_ref[...])
 
     table = table_ref[...]
     sub = lax.broadcasted_iota(jnp.int32, table.shape, 2)
@@ -227,7 +261,7 @@
     sub = sub.reshape(-1, 256)
     for bit in (1, 2, 4):
         flat = jnp.where((sub & bit) != 0, pltpu.roll(flat, bit, 1), flat)
-    binned = jnp.sum(flat.reshape(table.shape[0] * HEADS, PAD, 256), axis=1)
+    binned = jnp.sum(flat.reshape(HEADS * table.shape[1], PAD, 256), axis=1)
 
     pieces_ref[...] = jnp.zeros_like(pieces_ref)
     count = 0
@@ -244,31 +278,6 @@
     pieces_ref[count, 0:1, :] = gain_low[:, :128]
     pieces_ref[count, 1:2, : channels - 128] = gain_low[:, 128:]
 
-
-def finish_kernel(
-    nlat, nlon, res_ref, own_ref, pieces_ref,
-    both_ref, qkv_ref, proj_ref, table_ref, gain_ref,
-    land_ref, rs1_ref, mid_ref, rs2_ref, ag2_ref, ag_ref, grad_ref,
-    sends, recvs, lon_send, lon_recv, lat_send, lat_recv,
-):
-    lat = lax.axis_index("lat")
-    lon = lax.axis_index("lon")
-    chunk = mid_ref.shape[0]
-    share = chunk // nlat
-    last = own_ref.shape[1] - 1
-    down, right = lax.rem(lat + 1, nlat), lax.rem(lon + 1, nlon)
-    up, left = lax.rem(lat + nlat - 1, nlat), lax.rem(lon + nlon - 1, nlon)
-
-    barrier = pltpu.get_barrier_semaphore()
-    for step in range(1, nlon):
-        who = (lat, lax.rem(lon + step, nlon))
-        pl.semaphore_signal(barrier, inc=1, device_id=who, device_id_type=MESH)
-    for step in range(1, nlat):
-        who = (lax.rem(lat + step, nlat), lon)
-        pl.semaphore_signal(barrier, inc=1, device_id=who, device_id_type=MESH)
-    pl.semaphore_signal(barrier, inc=1, device_id=(up, left), device_id_type=MESH)
-    pl.semaphore_wait(barrier, nlon + nlat - 1)
-
     def along_lon(src, dst, which, step):
         return pltpu.make_async_remote_copy(
             src_ref=src, dst_ref=dst, send_sem=lon_send.at[which], recv_sem=lon_recv.at[which],
@@ -289,23 +298,6 @@
             rs1_ref.at[pl.ds((step - 1) * chunk, chunk)], 0, step,
         ).start()
 
-    top = pl.ds(0, HALF_LAT)
-    bottom = pl.ds(HALF_LAT, HALF_LAT)
-    moves = (
-        (res_ref.at[top, pl.ds(0, last)], land_ref.at[top, pl.ds(1, last)], (down, lon)),
-        (res_ref.at[top, pl.ds(last, 1)], land_ref.at[top, pl.ds(0, 1)], (down, right)),
-        (res_ref.at[bottom, pl.ds(last, 1)], land_ref.at[bottom, pl.ds(0, 1)], (lat, right)),
-    )
-    copies = [
-        pltpu.make_async_remote_copy(
-            src_ref=src, dst_ref=dst, send_sem=sends.at[i], recv_sem=recvs.at[i],
-            device_id=who, device_id_type=MESH,
-        )
-        for i, (src, dst, who) in enumerate(moves)
-    ]
-    for copy in copies:
-        copy.start()
-
     own_part = own_ref[bottom, 1:].astype(f32) + res_ref[bottom, :last].astype(f32)
     both_ref[bottom, 1:] = own_part.astype(bf16)
 
@@ -324,10 +316,10 @@
         ).start()
 
     pltpu.make_async_copy(rs2_ref, rs2_ref, lat_recv.at[0]).wait()
-    total = mid_ref[pl.ds(lat * share, share)].astype(f32)
+    final = mid_ref[pl.ds(lat * share, share)].astype(f32)
     for step in range(nlat - 1):
-        total = total + rs2_ref[step * share : (step + 1) * share].astype(f32)
-    ag2_ref[pl.ds(lat * share, share)] = total.astype(bf16)
+        final = final + rs2_ref[step * share : (step + 1) * share].astype(f32)
+    ag2_ref[pl.ds(lat * share, share)] = final.astype(bf16)
 
     @pl.loop(1, nlat)
     def _(step):
@@ -350,13 +342,12 @@
     ).astype(bf16)
 
     pltpu.make_async_copy(rs1_ref, rs1_ref, lon_recv.at[1]).wait()
-    channels = gain_ref.shape[1]
     at = 0
     for column in range(4 * channels // 128):
         part = ag_ref[at : at + channels // ROWS].astype(f32)
         grad_ref[:, column * 128 : (column + 1) * 128] = part.reshape(channels, 128)
         at += channels // ROWS
-    kinds, heads, extent = table_ref.shape
+    heads, kinds, extent = table_out.shape
     rows_t = kinds * heads // ROWS
     sides = []
     for side in range(2):
@@ -370,20 +361,22 @@
         mean = jnp.sum(jnp.sum(value * value, axis=1, keepdims=True), axis=0, keepdims=True)
         return jnp.minimum(1.0, lax.rsqrt(mean * (1.0 / entries) + clip_eps))
 
-    wide = grad_ref[:, : 3 * channels]
-    qkv_ref[...] = wide * scale(wide, wide.size)
+    big = grad_ref[:, : 3 * channels]
+    qkv_out[...] = big * scale(big, big.size)
     proj = grad_ref[:, 3 * channels :]
-    proj_ref[...] = proj * scale(proj, proj.size)
+    proj_out[...] = proj * scale(proj, proj.size)
     lane = lax.broadcasted_iota(jnp.int32, table.shape, 1)
     table = jnp.where(lane < extent, table, 0.0)
     table = table * scale(table, kinds * heads * extent)
-    for kind in range(kinds):
-        table_ref[kind] = table[kind * heads : (kind + 1) * heads, :extent]
-    gain_ref[...] = gain * scale(gain, channels)
+    for h in range(heads):
+        table_out[h] = table[h * kinds : (h + 1) * kinds, :extent]
+    gain_out[...] = gain * scale(gain, channels)
 
     for which in range(2):
         pltpu.make_async_copy(rs1_ref, rs1_ref, lon_send.at[which]).wait()
         pltpu.make_async_copy(rs2_ref, rs2_ref, lat_send.at[which]).wait()
+    for copy in fetch:
+        copy.wait_send()
 
 
 def on_device(nlat, nlon, state_grid, norm_gain, w_qkv, w_proj, bias_table, window_kind, cotangent):
@@ -397,36 +390,28 @@
     joint = jnp.pad(joint, ((0, 0), (0, 0), (0, PAD - HALF_LON), (0, 0)))
     grid_shape = joint.shape
 
-    block = pl.pallas_call(
-        functools.partial(halo_kernel, nlat, nlon),
-        name="halo",
-        out_shape=jax.ShapeDtypeStruct(grid_shape, bf16),
-        in_specs=[VM],
-        out_specs=VM,
-        scratch_shapes=[
-            pltpu.SemaphoreType.DMA((3,)),
-            pltpu.SemaphoreType.DMA((3,)),
-            pltpu.SemaphoreType.DMA(()),
-        ],
-        compiler_params=pltpu.CompilerParams(collective_id=0, has_side_effects=True),
-    )(joint)
-
     wide = 2 * PAD
     four = (WIN_LAT, windows, wide)
     total = WIN_LAT * windows * wide
     tokens = WIN_LAT * wide
     used = 4 * channels // 128 * (channels // ROWS) + 2 * (kinds * heads // ROWS) + 1
     share = -(-used // devices)
-    res, pieces = pl.pallas_call(
-        attend_kernel,
-        name="attend",
+    both, qkv_grad, proj_grad, table_grad, gain_grad = pl.pallas_call(
+        functools.partial(block_kernel, nlat, nlon),
+        name="block",
         out_shape=(
-            jax.ShapeDtypeStruct(four + (2 * channels,), bf16),
-            jax.ShapeDtypeStruct((share * devices, ROWS, 128), bf16),
+            jax.ShapeDtypeStruct(grid_shape, bf16),
+            jax.ShapeDtypeStruct((channels, 3 * channels), f32),
+            jax.ShapeDtypeStruct((channels, channels), f32),
+            jax.ShapeDtypeStruct((heads, kinds, extent), f32),
+            jax.ShapeDtypeStruct((1, channels), f32),
         ),
         in_specs=[pl.BlockSpec(memory_space=pltpu.SMEM)] + [VM] * 5,
-        out_specs=(VM, VM),
+        out_specs=(VM,) * 5,
         scratch_shapes=[
+            pltpu.VMEM(grid_shape, bf16),
+            pltpu.VMEM(grid_shape, bf16),
+            pltpu.VMEM((share * devices, ROWS, 128), bf16),
             pltpu.VMEM((total, channels), f32),
             pltpu.VMEM((total, 1), f32),
             pltpu.VMEM((total, channels), bf16),
@@ -437,39 +422,18 @@
             pltpu.VMEM(four + (3 * channels,), bf16),
             pltpu.VMEM((tokens, 128), f32),
             pltpu.VMEM((128, tokens), bf16),
-            pltpu.VMEM((kinds, heads, 256), f32),
-            pltpu.VMEM((kinds, heads, PAD, 256), f32),
+            pltpu.VMEM((heads, kinds, 256), f32),
+            pltpu.VMEM((heads, kinds, PAD, 256), f32),
             pltpu.VMEM((channels, 4 * channels), f32),
-        ],
-    )(
-        window_kind,
-        block.reshape(four + (2 * channels,)),
-        norm_gain.reshape(1, channels),
-        w_qkv,
-        w_proj,
-        bias_table,
-    )
-
-    both, qkv_grad, proj_grad, table_grad, gain_grad = pl.pallas_call(
-        functools.partial(finish_kernel, nlat, nlon),
-        name="finish",
-        out_shape=(
-            jax.ShapeDtypeStruct(grid_shape, bf16),
-            jax.ShapeDtypeStruct((channels, 3 * channels), f32),
-            jax.ShapeDtypeStruct((channels, channels), f32),
-            jax.ShapeDtypeStruct((kinds, heads, extent), f32),
-            jax.ShapeDtypeStruct((1, channels), f32),
-        ),
-        in_specs=[VM] * 3,
-        out_specs=(VM,) * 5,
-        scratch_shapes=[
             pltpu.VMEM(grid_shape, bf16),
             pltpu.VMEM((share * nlat * (nlon - 1), ROWS, 128), bf16),
             pltpu.VMEM((share * nlat, ROWS, 128), bf16),
             pltpu.VMEM((share * (nlat - 1), ROWS, 128), bf16),
             pltpu.VMEM((share * nlat, ROWS, 128), bf16),
             pltpu.VMEM((share * devices, ROWS, 128), bf16),
-            pltpu.VMEM((channels, 4 * channels), f32),
+            pltpu.SemaphoreType.DMA((3,)),
+            pltpu.SemaphoreType.DMA((3,)),
+            pltpu.SemaphoreType.DMA(()),
             pltpu.SemaphoreType.DMA((3,)),
             pltpu.SemaphoreType.DMA((3,)),
             pltpu.SemaphoreType.DMA((2,)),
@@ -477,8 +441,15 @@
             pltpu.SemaphoreType.DMA((2,)),
             pltpu.SemaphoreType.DMA((2,)),
         ],
-        compiler_params=pltpu.CompilerParams(collective_id=1, has_side_effects=True),
-    )(res.reshape(grid_shape), joint, pieces)
+        compiler_params=pltpu.CompilerParams(collective_id=0, has_side_effects=True),
+    )(
+        window_kind,
+        joint,
+        norm_gain.reshape(1, channels),
+        w_qkv,
+        w_proj,
+        bias_table.transpose(1, 0, 2),
+    )
 
     both = both[:, :, :HALF_LON].reshape(rows_dev, cols_dev, 2 * channels)
     return (
@@ -486,7 +457,7 @@
         both[:, :, channels:],
         qkv_grad,
         proj_grad,
-        table_grad,
+        table_grad.transpose(1, 0, 2),
         gain_grad.reshape(channels),
     )
 

time: 67.1 us -> 59 us (0.88)
  Pallas kernels: 57 us -> 50.3 us
  local copies, waits for them, and re-layouts: 7.79 us -> 6.42 us
    pallas_call x3 -> x1, Pallas kernels: 57 us -> 50.3 us  [on_device(): pl.pallas_call(functools.partial(block_kernel, nlat, nlon), name='block',...]
    unnamed x13 -> x12, local copies, waits for them, and re-layouts: 4.71 us -> 3.36 us
where the time goes in v3:
time: 59 us; the launch traced here: 58.6 us
  Pallas kernels  50.3 us (85%)
  local copies, waits for them, and re-layouts  6.42 us (11%)
  other arithmetic  1.19 us (2%)
  between operations  0.67 us (1%)
    pallas_call x1, Pallas kernels, on_device(): pl.pallas_call(functools.partial(block_kernel, nlat, nlon), name='block',...  50.3 us
    unnamed x12, local copies, waits for them, and re-layouts  3.36 us
    concatenate x1, other arithmetic, on_device(): joint = jnp.concatenate([state_grid, cotangent], axis=2)  1.19 us

profile of v3, /device:TPU:0, one launch (start us, length us, event | category | flops | bytes accessed | tf_op | source)
XLA Modules:
  0.0 58.6 jit_solution(7223537941656402541)
XLA Ops:
  0.6 1.2 %pad_maximum_fusion = bf16[6,84,384]{2,1,0:T(8,128)(2,1)S(1)} fusion(bf16[6,84,192]{2,1,0:T(8,128)(2,1)} %param.13, bf16[6,84,192]{2,1,0:T(8,128)(2,1)} %param.7), kind=kLoop, calls=%fused_computation | loop fusion | flops 774144 | bytes 774144 | tf_op jit(solution)/shard_map/concatenate | solution.py:388
  1.8 0.1 reshape.24
  2.0 0.9 %pad.4.own_ref = bf16[6,14,8,384]{3,2,1,0:T(8,128)(2,1)} pad(bf16[6,14,6,384]{3,2,1,0:T(8,128)(2,1)S(1)} %reshape.24, bf16[]{:T(256)} %constant.2.clone.1), padding=0_0x0_0x0_2x0_0 | pad | bytes 903170 | tf_op jit(solution)/shard_map/jit(_pad)/pad | solution.py:390
  2.8 50.3 %block.1 = (bf16[6,14,8,384]{3,2,1,0:T(8,128)(2,1)}, f32[192,576]{1,0:T(8,128)}, f32[192,192]{1,0:T(8,128)}, f32[6,8,253]{2,1,0:T(8,128)}, f32[1,192]{1,0:T(1,128)}) custom-call(s32[4,56]{1,0:T(4,128)} %kinds_ref.1, bf16[6,14,8,384]{3,2,1,0:T(8,128)(2,1)} %pad.4.own_ref, f32[1,192]{1,0:T(1,128)} %bitcast.9, bf16[192,576]{1,0:T(8,128)(2,1)} %wqkv_ref.1, ...), custom_call_target="tpu_custom_call" | custom-call | tf_op jit(solution)/shard_map/block/pallas_call | solution.py:399
  53.2 1.2 %reshape.26 = bf16[6,84,384]{2,1,0:T(8,128)(2,1)S(1)} reshape(bf16[6,14,6,384]{3,2,1,0:T(8,128)(2,1)} %bitcast.5) | data formatting | bytes 774144 | tf_op jit(solution)/shard_map/reshape | solution.py:454
  54.3 0.0 copy-start
  54.4 0.9 %fusion = (bf16[6,84,192]{2,1,0:T(8,128)(2,1)}, bf16[6,84,192]{2,1,0:T(8,128)(2,1)}) fusion(bf16[6,84,384]{2,1,0:T(8,128)(2,1)S(1)} %reshape.26), kind=kLoop, calls=%fused_computation.1 | loop fusion | bytes 774144 | tf_op jit(solution)/shard_map/slice | solution.py:457
  55.2 0.2 copy-done
  55.5 0.0 copy-start.1
  55.5 0.8 %copy.17 = f32[192,576]{1,0:T(8,128)} copy(f32[192,576]{1,0:T(8,128)S(1)} %copy-done) | data formatting | bytes 884736
  56.3 0.3 copy-done.1
  56.6 0.0 copy-start.2
  56.6 0.7 %copy.18 = f32[192,192]{1,0:T(8,128)} copy(f32[192,192]{1,0:T(8,128)S(1)} %copy-done.1) | data formatting | bytes 294912
  57.3 0.1 copy-done.2
  57.4 0.0 copy-start.3
  57.4 0.6 %copy.19 = f32[8,6,253]{2,0,1:T(8,128)} copy(f32[8,6,253]{2,0,1:T(8,128)S(1)} %bitcast.7) | data formatting | bytes 97152
  58.0 0.0 copy-done.3
  58.0 0.6 copy.20
Async XLA Ops:
  54.3 1.1 %copy-start = (f32[192,576]{1,0:T(8,128)S(1)}, f32[192,576]{1,0:T(8,128)}, u32[]{:S(2)}) copy-start(f32[192,576]{1,0:T(8,128)} %get-tuple-element.26) | copy-start | bytes 1327108
  55.5 1.1 %copy-start.1 = (f32[192,192]{1,0:T(8,128)S(1)}, f32[192,192]{1,0:T(8,128)}, u32[]{:S(2)}) copy-start(f32[192,192]{1,0:T(8,128)} %get-tuple-element.27) | copy-start | bytes 442372
  56.6 0.8 %copy-start.2 = (f32[6,8,253]{2,1,0:T(8,128)S(1)}, f32[6,8,253]{2,1,0:T(8,128)}, u32[]{:S(2)}) copy-start(f32[6,8,253]{2,1,0:T(8,128)} %get-tuple-element.14) | copy-start | bytes 145732
  57.4 0.7 %copy-start.3 = (f32[1,192]{1,0:T(1,128)S(1)}, f32[1,192]{1,0:T(1,128)}, u32[]{:S(2)}) copy-start(f32[1,192]{1,0:T(1,128)} %get-tuple-element.15) | copy-start | bytes 2308

commit v4 on v3

--- a/solution.py
+++ b/solution.py
@@ -45,7 +45,7 @@
     unit_ref, inv_ref, normed_ref, qkv_ref, dmix_ref, g_ref, mixed_ref, dqkv_ref,
     neg_ref, emb_ref, table_in, table_ref, grad_ref,
     land_ref, rs1_ref, mid_ref, rs2_ref, ag2_ref, ag_ref,
-    halo_send, halo_recv, local, sends, recvs, lon_send, lon_recv, lat_send, lat_recv,
+    halo_send, halo_recv, row_send, row_recv, local, sends, recvs, lon_send, lon_recv, lat_send, lat_recv,
 ):
     lat = lax.axis_index("lat")
     lon = lax.axis_index("lon")
@@ -80,8 +80,8 @@
     inner = pl.ds(1, last)
     moves = (
         (own_ref.at[bottom, pl.ds(0, 1)], block_ref.at[bottom, pl.ds(last, 1)], (lat, left)),
-        (own_ref.at[top, inner], block_ref.at[top, pl.ds(0, last)], (up, lon)),
         (own_ref.at[top, pl.ds(0, 1)], block_ref.at[top, pl.ds(last, 1)], (up, left)),
+        (own_ref.at[top, pl.ds(last, 1)], block_ref.at[top, pl.ds(last - 1, 1)], (up, lon)),
     )
     fetch = [
         pltpu.make_async_remote_copy(
@@ -90,8 +90,22 @@
         )
         for i, (src, dst, who) in enumerate(moves)
     ]
+
+    def fetch_rows(w):
+        return pltpu.make_async_remote_copy(
+            src_ref=own_ref.at[top, pl.ds(2 * w + 1, 2)],
+            dst_ref=block_ref.at[top, pl.ds(2 * w, 2)],
+            send_sem=row_send.at[w], recv_sem=row_recv.at[w],
+            device_id=(up, lon), device_id_type=MESH,
+        )
+
     for copy in fetch:
         copy.start()
+
+    @pl.loop(0, windows - 1)
+    def _(w):
+        fetch_rows(w).start()
+
     keep = pltpu.make_async_copy(
         own_ref.at[bottom, inner], block_ref.at[bottom, pl.ds(0, last)], local
     )
@@ -100,20 +114,37 @@
     def prepare(first):
         here = slice(first, first + HALF_LAT)
         count = HALF_LAT * windows * wide
-        rows = slice(first * windows * wide, first * windows * wide + count)
         three = (HALF_LAT, windows, wide)
         x = block_ref[here, :, :, :channels].astype(f32).reshape(count, channels)
         g = block_ref[here, :, :, channels:].astype(f32).reshape(count, channels).astype(bf16)
-        g_ref[rows] = g
+        g_ref[here] = g.reshape(three + (channels,))
         centre = x - jnp.mean(x, axis=-1, keepdims=True)
         inverse = lax.rsqrt(jnp.mean(centre * centre, axis=-1, keepdims=True) + norm_eps)
         unit = centre * inverse
-        unit_ref[rows] = unit
-        inv_ref[rows] = inverse
+        unit_ref[here] = unit.reshape(three + (channels,))
+        inv_ref[here] = inverse.reshape(three + (1,))
         normed = (unit * gain_ref[...]).astype(bf16)
-        normed_ref[rows] = normed
+        normed_ref[here] = normed.reshape(three + (channels,))
         qkv_ref[here] = nn(normed, wqkv_ref[...]).astype(bf16).reshape(three + (3 * channels,))
         dmix_ref[here] = nt(g, wproj_ref[...]).astype(bf16).reshape(three + (channels,))
+
+    def prepare_window(w):
+        here = slice(0, HALF_LAT)
+        count = HALF_LAT * wide
+        three = (HALF_LAT, wide)
+        pair = pl.ds(2 * w, 2)
+        x = block_ref[here, pair, :, :channels].astype(f32).reshape(count, channels)
+        g = block_ref[here, pair, :, channels:].astype(f32).reshape(count, channels).astype(bf16)
+        g_ref[here, w] = g.reshape(three + (channels,))
+        centre = x - jnp.mean(x, axis=-1, keepdims=True)
+        inverse = lax.rsqrt(jnp.mean(centre * centre, axis=-1, keepdims=True) + norm_eps)
+        unit = centre * inverse
+        unit_ref[here, w] = unit.reshape(three + (channels,))
+        inv_ref[here, w] = inverse.reshape(three + (1,))
+        normed = (unit * gain_ref[...]).astype(bf16)
+        normed_ref[here, w] = normed.reshape(three + (channels,))
+        qkv_ref[here, w] = nn(normed, wqkv_ref[...]).astype(bf16).reshape(three + (3 * channels,))
+        dmix_ref[here, w] = nt(g, wproj_ref[...]).astype(bf16).reshape(three + (channels,))
 
     def place(index):
         slot = index >> 4
@@ -144,7 +175,6 @@
     prepare(HALF_LAT)
     fetch[1].wait_recv()
     fetch[2].wait_recv()
-    prepare(0)
 
     lane8 = lax.broadcasted_iota(jnp.int32, (PAD, 128), 1)
     kind_of = lax.broadcasted_iota(jnp.int32, (bias_ref.shape[1], PAD, 256), 0)
@@ -159,6 +189,11 @@
 
     @pl.loop(0, windows)
     def _(w):
+        @pl.when(w < windows - 1)
+        def _():
+            fetch_rows(w).wait_recv()
+
+        prepare_window(w)
         kind = kinds_ref[lat, lon * windows + w]
         qkv = qkv_ref[:, w].reshape(tokens, 3 * channels)
         queries = qkv[:, :channels]
@@ -227,9 +262,9 @@
     d_qkv = dqkv_ref[...].reshape(total, 3 * channels)
     branch = nn(mixed, wproj_ref[...])
     d_normed = nt(d_qkv, wqkv_ref[...])
-    unit = unit_ref[...]
+    unit = unit_ref[...].reshape(total, channels)
     d_unit = d_normed * gain_ref[...]
-    path = inv_ref[...] * (
+    path = inv_ref[...].reshape(total, 1) * (
         d_unit
         - jnp.mean(d_unit, axis=-1, keepdims=True)
         - unit * jnp.mean(d_unit * unit, axis=-1, keepdims=True)
@@ -252,8 +287,8 @@
     ]
     for copy in copies:
         copy.start()
-    grad_ref[:, : 3 * channels] = tn(normed_ref[...], d_qkv)
-    grad_ref[:, 3 * channels :] = tn(mixed, g_ref[...])
+    grad_ref[:, : 3 * channels] = tn(normed_ref[...].reshape(total, channels), d_qkv)
+    grad_ref[:, 3 * channels :] = tn(mixed, g_ref[...].reshape(total, channels))
 
     table = table_ref[...]
     sub = lax.broadcasted_iota(jnp.int32, table.shape, 2)
@@ -378,6 +413,10 @@
     for copy in fetch:
         copy.wait_send()
 
+    @pl.loop(0, windows - 1)
+    def _(w):
+        fetch_rows(w).wait_send()
+
 
 def on_device(nlat, nlon, state_grid, norm_gain, w_qkv, w_proj, bias_table, window_kind, cotangent):
     rows_dev, cols_dev, channels = state_grid.shape
@@ -392,7 +431,6 @@
 
     wide = 2 * PAD
     four = (WIN_LAT, windows, wide)
-    total = WIN_LAT * windows * wide
     tokens = WIN_LAT * wide
     used = 4 * channels // 128 * (channels // ROWS) + 2 * (kinds * heads // ROWS) + 1
     share = -(-used // devices)
@@ -412,12 +450,12 @@
             pltpu.VMEM(grid_shape, bf16),
             pltpu.VMEM(grid_shape, bf16),
             pltpu.VMEM((share * devices, ROWS, 128), bf16),
-            pltpu.VMEM((total, channels), f32),
-            pltpu.VMEM((total, 1), f32),
-            pltpu.VMEM((total, channels), bf16),
+            pltpu.VMEM(four + (channels,), f32),
+            pltpu.VMEM(four + (1,), f32),
+            pltpu.VMEM(four + (channels,), bf16),
             pltpu.VMEM(four + (3 * channels,), bf16),
             pltpu.VMEM(four + (channels,), bf16),
-            pltpu.VMEM((total, channels), bf16),
+            pltpu.VMEM(four + (channels,), bf16),
             pltpu.VMEM(four + (channels,), bf16),
             pltpu.VMEM(four + (3 * channels,), bf16),
             pltpu.VMEM((tokens, 128), f32),
@@ -433,6 +471,8 @@
             pltpu.VMEM((share * devices, ROWS, 128), bf16),
             pltpu.SemaphoreType.DMA((3,)),
             pltpu.SemaphoreType.DMA((3,)),
+            pltpu.SemaphoreType.DMA((windows - 1,)),
+            pltpu.SemaphoreType.DMA((windows - 1,)),
             pltpu.SemaphoreType.DMA(()),
             pltpu.SemaphoreType.DMA((3,)),
             pltpu.SemaphoreType.DMA((3,)),

time: 59 us -> 55.9 us (0.947)
  Pallas kernels: 50.3 us -> 47.3 us
    pallas_call x1, Pallas kernels: 50.3 us -> 47.3 us  [on_device(): pl.pallas_call(functools.partial(block_kernel, nlat, nlon), name='block',...]
where the time goes in v4:
time: 55.9 us; the launch traced here: 55.5 us
  Pallas kernels  47.3 us (85%)
  local copies, waits for them, and re-layouts  6.42 us (11%)
  other arithmetic  1.19 us (2%)
  between operations  0.67 us (1%)
    pallas_call x1, Pallas kernels, on_device(): pl.pallas_call(functools.partial(block_kernel, nlat, nlon), name='block',...  47.3 us
    unnamed x12, local copies, waits for them, and re-layouts  3.36 us
    concatenate x1, other arithmetic, on_device(): joint = jnp.concatenate([state_grid, cotangent], axis=2)  1.19 us
    reshape x1, local copies, waits for them, and re-layouts, on_device(): both = both[:, :, :HALF_LON].reshape(rows_dev, cols_dev, 2 * channels)  1.17 us

profile of v4, /device:TPU:0, one launch (start us, length us, event | category | flops | bytes accessed | tf_op | source)
XLA Modules:
  0.0 55.5 jit_solution(4422341186863346709)
XLA Ops:
  0.6 1.2 %pad_maximum_fusion = bf16[6,84,384]{2,1,0:T(8,128)(2,1)S(1)} fusion(bf16[6,84,192]{2,1,0:T(8,128)(2,1)} %param.13, bf16[6,84,192]{2,1,0:T(8,128)(2,1)} %param.7), kind=kLoop, calls=%fused_computation | loop fusion | flops 774144 | bytes 774144 | tf_op jit(solution)/shard_map/concatenate | solution.py:427
  1.8 0.1 reshape.24
  2.0 0.9 %pad.4.own_ref = bf16[6,14,8,384]{3,2,1,0:T(8,128)(2,1)} pad(bf16[6,14,6,384]{3,2,1,0:T(8,128)(2,1)S(1)} %reshape.24, bf16[]{:T(256)} %constant.2.clone.1), padding=0_0x0_0x0_2x0_0 | pad | bytes 903170 | tf_op jit(solution)/shard_map/jit(_pad)/pad | solution.py:429
  2.8 47.3 %block.1 = (bf16[6,14,8,384]{3,2,1,0:T(8,128)(2,1)}, f32[192,576]{1,0:T(8,128)}, f32[192,192]{1,0:T(8,128)}, f32[6,8,253]{2,1,0:T(8,128)}, f32[1,192]{1,0:T(1,128)}) custom-call(s32[4,56]{1,0:T(4,128)} %kinds_ref.1, bf16[6,14,8,384]{3,2,1,0:T(8,128)(2,1)} %pad.4.own_ref, f32[1,192]{1,0:T(1,128)} %bitcast.9, bf16[192,576]{1,0:T(8,128)(2,1)} %wqkv_ref.1, ...), custom_call_target="tpu_custom_call" | custom-call | tf_op jit(solution)/shard_map/block/pallas_call | solution.py:437
  50.1 1.2 %reshape.26 = bf16[6,84,384]{2,1,0:T(8,128)(2,1)S(1)} reshape(bf16[6,14,6,384]{3,2,1,0:T(8,128)(2,1)} %bitcast.5) | data formatting | bytes 774144 | tf_op jit(solution)/shard_map/reshape | solution.py:494
  51.3 0.0 copy-start
  51.3 0.9 %fusion = (bf16[6,84,192]{2,1,0:T(8,128)(2,1)}, bf16[6,84,192]{2,1,0:T(8,128)(2,1)}) fusion(bf16[6,84,384]{2,1,0:T(8,128)(2,1)S(1)} %reshape.26), kind=kLoop, calls=%fused_computation.1 | loop fusion | bytes 774144 | tf_op jit(solution)/shard_map/slice | solution.py:497
  52.2 0.2 copy-done
  52.4 0.0 copy-start.1
  52.4 0.8 %copy.17 = f32[192,576]{1,0:T(8,128)} copy(f32[192,576]{1,0:T(8,128)S(1)} %copy-done) | data formatting | bytes 884736
  53.2 0.3 copy-done.1
  53.5 0.0 copy-start.2
  53.5 0.7 %copy.18 = f32[192,192]{1,0:T(8,128)} copy(f32[192,192]{1,0:T(8,128)S(1)} %copy-done.1) | data formatting | bytes 294912
  54.2 0.1 copy-done.2
  54.3 0.0 copy-start.3
  54.3 0.6 %copy.19 = f32[8,6,253]{2,0,1:T(8,128)} copy(f32[8,6,253]{2,0,1:T(8,128)S(1)} %bitcast.7) | data formatting | bytes 97152
  54.9 0.0 copy-done.3
  55.0 0.6 %copy.20 = f32[192]{0:T(256)} copy(f32[192]{0:T(256)S(1)} %bitcast.8) | data formatting | bytes 1536
Async XLA Ops:
  51.3 1.1 %copy-start = (f32[192,576]{1,0:T(8,128)S(1)}, f32[192,576]{1,0:T(8,128)}, u32[]{:S(2)}) copy-start(f32[192,576]{1,0:T(8,128)} %get-tuple-element.26) | copy-start | bytes 1327108
  52.4 1.1 %copy-start.1 = (f32[192,192]{1,0:T(8,128)S(1)}, f32[192,192]{1,0:T(8,128)}, u32[]{:S(2)}) copy-start(f32[192,192]{1,0:T(8,128)} %get-tuple-element.27) | copy-start | bytes 442372
  53.5 0.8 %copy-start.2 = (f32[6,8,253]{2,1,0:T(8,128)S(1)}, f32[6,8,253]{2,1,0:T(8,128)}, u32[]{:S(2)}) copy-start(f32[6,8,253]{2,1,0:T(8,128)} %get-tuple-element.14) | copy-start | bytes 145732
  54.3 0.7 %copy-start.3 = (f32[1,192]{1,0:T(1,128)S(1)}, f32[1,192]{1,0:T(1,128)}, u32[]{:S(2)}) copy-start(f32[1,192]{1,0:T(1,128)} %get-tuple-element.15) | copy-start | bytes 2308
